TPU v7x, 32 devices: a whole 2x2x4 slice. The times are simulated.
32 devices in a mesh: grp: 4 (over x, core), dp: 8 (over z, y).
Axes of the slice: x: 2, y: 2, z: 4, core: 2. Of those that a mesh axis runs over, the one named last changes fastest.
Arguments:
- inputs: bfloat16 [32, 256, 768], P(('grp', 'dp')), may hold values from -36 to 36
- segment_ids: int32 [32, 256], P(('grp', 'dp')), may hold values from 0 to 4, never falling along the last dimension, each value on 1 to 128 neighbouring positions
- out_grad: bfloat16 [32, 256, 768], P(('grp', 'dp')), may hold values from -6 to 6
- norm_gain: float32 [768], P('grp'), may hold values from 0.4 to 4, as said below
- in_weight: float32 [768, 3352], P('grp'), may hold values from -0.21875 to 0.21875
- conv_params: float32 [5, 1792], P(None, 'grp'), may hold values from -3 to 3
- head_params: float32 [3, 24], P(None, 'grp'), may hold values from -7 to 2.8
- gate_gain: float32 [1536], P('grp'), may hold values from 0.4 to 4, as said below
- out_weight: float32 [1536, 768], P('grp'), may hold values from -0.15625 to 0.15625
- norm_gain_moments: float32 [2, 768], P(None, 'grp'), may hold values from -0.12 to 0.12, as said below
- in_weight_moments: float32 [2, 768, 3352], P(None, 'grp'), may hold values from -0.015 to 0.015, as said below
- conv_params_moments: float32 [2, 5, 1792], P(None, None, 'grp'), may hold values from -0.045 to 0.045, as said below
- head_params_moments: float32 [2, 3, 24], P(None, None, 'grp'), may hold values from -0.06 to 0.06, as said below
- gate_gain_moments: float32 [2, 1536], P(None, 'grp'), may hold values from -0.045 to 0.045, as said below
- out_weight_moments: float32 [2, 1536, 768], P(None, 'grp'), may hold values from -0.015 to 0.015, as said below
Outputs:
- block_out: bfloat16 [32, 256, 768], P(('grp', 'dp'))
- input_grad: float32 [32, 256, 768], P(('grp', 'dp'))
- norm_gain_grad: float32 [768], P('grp')
- in_weight_grad: float32 [768, 3352], P('grp')
- conv_params_grad: float32 [5, 1792], P(None, 'grp')
- head_params_grad: float32 [3, 24], P(None, 'grp')
- gate_gain_grad: float32 [1536], P('grp')
- out_weight_grad: float32 [1536, 768], P('grp')
- new_norm_gain: float32 [768], P('grp')
- new_in_weight: float32 [768, 3352], P('grp')
- new_conv_params: float32 [5, 1792], P(None, 'grp')
- new_head_params: float32 [3, 24], P(None, 'grp')
- new_gate_gain: float32 [1536], P('grp')
- new_out_weight: float32 [1536, 768], P('grp')
- new_norm_gain_moments: float32 [2, 768], P(None, 'grp')
- new_in_weight_moments: float32 [2, 768, 3352], P(None, 'grp')
- new_conv_params_moments: float32 [2, 5, 1792], P(None, None, 'grp')
- new_head_params_moments: float32 [2, 3, 24], P(None, None, 'grp')
- new_gate_gain_moments: float32 [2, 1536], P(None, 'grp')
- new_out_weight_moments: float32 [2, 1536, 768], P(None, 'grp')
Inputs may be any that keep to these rules, and one draw needn't show every extreme that they name: `segment_ids`: within each sequence the ids never fall, and no document spans more than 128 positions. `norm_gain`: every entry is positive. `gate_gain`: every entry is positive. `norm_gain_moments`: every entry of row 1 is positive. `in_weight_moments`: every entry of row 1 is positive. `conv_params_moments`: every entry of row 1 is positive. `head_params_moments`: every entry of row 1 is positive. `gate_gain_moments`: every entry of row 1 is positive. `out_weight_moments`: every entry of row 1 is positive.
All inputs are finite; a program needn't handle non-finite values.
Results may differ from a plain program's by a relative error of at most 0.0014.
The roundings to bfloat16 on the way count: a program that leaves them out, or rounds other values in their place, can miss the bound.
Values may be sent and summed in bfloat16 or wider, within the bound.
A program may use at most 128 MiB of HBM per device.

v0:
```python
import jax
import jax.numpy as jnp
from jax import lax
from jax.sharding import PartitionSpec as P

STRETCH = 256
STEP = 5


norm_eps = 1e-05
clip_limit = 1.0
beta_first = 0.9
beta_second = 0.999
adam_eps = 1e-08
learn_rate = 0.02
weight_decay = 0.1


def norm_rows(features, gain_vec):
    inverse = lax.rsqrt(jnp.mean(features * features, axis=-1, keepdims=True) + norm_eps)
    return features * inverse * gain_vec


def scan_blocks(head_vals, step_size, log_rate, write_proj, read_proj, seg_row):
    highest = lax.Precision.HIGHEST
    length, head_count, head_width = head_vals.shape
    blocks = length // STRETCH
    block_vals = head_vals.reshape(blocks, STRETCH, head_count, head_width)
    step_heads = jnp.transpose(step_size.reshape(blocks, STRETCH, head_count), (0, 2, 1))
    log_cum = jnp.cumsum(
        jnp.transpose(log_rate.reshape(blocks, STRETCH, head_count), (0, 2, 1)), axis=2
    )
    write_blocks = write_proj.reshape(blocks, STRETCH, -1)
    read_blocks = read_proj.reshape(blocks, STRETCH, -1)
    seg_blocks = seg_row.reshape(blocks, STRETCH)
    positions = jnp.arange(STRETCH)
    causal = positions[:, None] >= positions[None, :]
    same_doc = (seg_blocks[:, :, None] == seg_blocks[:, None, :]) & causal[None]
    log_gap = jnp.where(
        same_doc[:, None], log_cum[:, :, :, None] - log_cum[:, :, None, :], -jnp.inf
    )
    scores = jnp.einsum("btn,bsn->bts", read_blocks, write_blocks, precision=highest)
    weighted = jnp.exp(log_gap) * scores[:, None] * step_heads[:, :, None, :]
    within = jnp.einsum("bhts,bshp->bthp", weighted, block_vals, precision=highest)
    end_same = (seg_blocks == seg_blocks[:, -1:]).astype(log_cum.dtype)
    to_end = jnp.exp(log_cum[:, :, -1:] - log_cum) * end_same[:, None, :] * step_heads
    block_states = jnp.einsum(
        "bhs,bshp,bsn->bhpn", to_end, block_vals, write_blocks, precision=highest
    )
    carried = block_states[0]
    outputs = [jnp.zeros_like(within[0])]
    return (within + jnp.stack(outputs)).reshape(length, head_count, head_width)


def mix_one(proj, conv_arr, head_arr, gate_arr, seg_row):
    length = proj.shape[0]
    inner_width = gate_arr.shape[0]
    head_count = head_arr.shape[1]
    conv_width = conv_arr.shape[1]
    kernel = conv_arr.shape[0] - 1
    state_width = (conv_width - inner_width) // 2
    gate_cols = proj[:, :inner_width]
    conv_input = proj[:, inner_width : inner_width + conv_width]
    step_raw = proj[:, inner_width + conv_width :]
    summed = conv_arr[kernel] + conv_arr[kernel - 1] * conv_input
    for offset in range(1, kernel):
        shifted = jnp.concatenate(
            [jnp.zeros((offset, conv_width), proj.dtype), conv_input[: length - offset]], axis=0
        )
        seg_before = jnp.concatenate(
            [jnp.full((offset,), -1, jnp.int32), seg_row[: length - offset]]
        )
        keep_mask = (seg_before == seg_row).astype(proj.dtype)[:, None]
        summed = summed + conv_arr[kernel - 1 - offset] * shifted * keep_mask
    activated = jax.nn.silu(summed)
    head_vals = activated[:, :inner_width].reshape(length, head_count, inner_width // head_count)
    write_proj = activated[:, inner_width : inner_width + state_width]
    read_proj = activated[:, inner_width + state_width :]
    step_size = jax.nn.softplus(step_raw + head_arr[0])
    log_rate = -step_size * jnp.exp(head_arr[1])
    scanned = scan_blocks(head_vals, step_size, log_rate, write_proj, read_proj, seg_row)
    scanned = scanned + head_arr[2][None, :, None] * head_vals
    gated = scanned.reshape(length, inner_width) * jax.nn.silu(gate_cols)
    return norm_rows(gated, gate_arr)


def adam_update(master, moments, grad_arr, clip_factor):
    clipped = grad_arr * clip_factor
    first = beta_first * moments[0] + (1.0 - beta_first) * clipped
    second_root = jnp.sqrt(
        beta_second * moments[1] * moments[1] + (1.0 - beta_second) * clipped * clipped
    )
    first_hat = first / (1.0 - beta_first**STEP)
    root_hat = second_root / jnp.sqrt(1.0 - beta_second**STEP)
    updated = master - learn_rate * (first_hat / (root_hat + adam_eps) + weight_decay * master)
    return (updated, jnp.stack([first, second_root]))


def square_sum(arrays):
    total = jnp.zeros((), jnp.float32)
    for grad_arr in arrays:
        total = total + jnp.sum(grad_arr * grad_arr)
    return total


def shards(
    inputs,
    segment_ids,
    out_grad,
    norm_gain,
    in_weight,
    conv_params,
    head_params,
    gate_gain,
    out_weight,
    norm_gain_moments,
    in_weight_moments,
    conv_params_moments,
    head_params_moments,
    gate_gain_moments,
    out_weight_moments,
):
    wide = jnp.float32
    half = jnp.bfloat16
    norm_half, in_half, conv_half, head_half, gate_half, out_half = (
        lax.all_gather(norm_gain.astype(half), "grp", axis=0, tiled=True),
        lax.all_gather(in_weight.astype(half), "grp", axis=0, tiled=True),
        lax.all_gather(conv_params.astype(half), "grp", axis=1, tiled=True),
        lax.all_gather(head_params.astype(half), "grp", axis=1, tiled=True),
        lax.all_gather(gate_gain.astype(half), "grp", axis=0, tiled=True),
        lax.all_gather(out_weight.astype(half), "grp", axis=0, tiled=True),
    )
    seq_count, length, width = inputs.shape
    row_count = seq_count * length
    input_wide = inputs.reshape(row_count, width).astype(wide)
    norm_wide = norm_half.astype(wide)
    conv_wide = conv_half.astype(wide)
    head_wide = head_half.astype(wide)
    gate_wide = gate_half.astype(wide)
    normed = norm_rows(input_wide, norm_wide).astype(half)
    proj = jnp.dot(normed, in_half, preferred_element_type=wide).reshape(seq_count, length, -1)

    def mixer(proj_arg, conv_arg, head_arg, gate_arg):
        return jax.vmap(
            lambda proj_row, seg_row: mix_one(proj_row, conv_arg, head_arg, gate_arg, seg_row)
        )(proj_arg, segment_ids)

    mixed_out, mixer_back = jax.vjp(mixer, proj, conv_wide, head_wide, gate_wide)
    mixed_half = mixed_out.reshape(row_count, -1).astype(half)
    block_rows = input_wide + jnp.dot(mixed_half, out_half, preferred_element_type=wide)
    block_out = block_rows.astype(half).reshape(seq_count, length, width)
    cotangent = out_grad.reshape(row_count, width)
    out_w_local = jnp.einsum("ti,td->id", mixed_half, cotangent, preferred_element_type=wide)
    d_mixed = jnp.einsum("td,id->ti", cotangent, out_half, preferred_element_type=wide)
    d_proj, grad_conv, grad_head, grad_gate = mixer_back(d_mixed.reshape(seq_count, length, -1))
    dproj_half = d_proj.reshape(row_count, -1).astype(half)
    grad_in_w = jnp.einsum("td,tk->dk", normed, dproj_half, preferred_element_type=wide)
    d_normed = jnp.einsum("tk,dk->td", dproj_half, in_half, preferred_element_type=wide)
    norm_back = jax.vjp(norm_rows, input_wide, norm_wide)[1]
    d_input, grad_norm = norm_back(d_normed)
    input_grad = (cotangent.astype(wide) + d_input).reshape(seq_count, length, width)
    all_owned = (
        lax.psum_scatter(grad_norm, "grp", scatter_dimension=0, tiled=True),
        lax.psum_scatter(grad_in_w, "grp", scatter_dimension=0, tiled=True),
        lax.psum_scatter(grad_conv, "grp", scatter_dimension=1, tiled=True),
        lax.psum_scatter(grad_head, "grp", scatter_dimension=1, tiled=True),
        lax.psum_scatter(grad_gate, "grp", scatter_dimension=0, tiled=True),
        lax.psum_scatter(out_w_local, "grp", scatter_dimension=0, tiled=True),
    )
    norm_grad, in_grad, conv_grad, head_grad, gate_grad, out_grad_w = lax.psum(
        (all_owned[0], all_owned[1], all_owned[2], all_owned[3], all_owned[4], all_owned[5]), "dp"
    )
    local_squares = square_sum((norm_grad, in_grad, conv_grad, head_grad, gate_grad, out_grad_w))
    squares = lax.psum(local_squares, "grp")
    clip_factor = jnp.minimum(1.0, clip_limit / jnp.sqrt(squares + 1e-06))
    norm_new, norm_mom = adam_update(norm_gain, norm_gain_moments, norm_grad, clip_factor)
    in_new, in_mom = adam_update(in_weight, in_weight_moments, in_grad, clip_factor)
    conv_new, conv_mom = adam_update(conv_params, conv_params_moments, conv_grad, clip_factor)
    head_new, head_mom = adam_update(head_params, head_params_moments, head_grad, clip_factor)
    gate_new, gate_mom = adam_update(gate_gain, gate_gain_moments, gate_grad, clip_factor)
    out_new, out_mom = adam_update(out_weight, out_weight_moments, out_grad_w, clip_factor)
    return (
        block_out,
        input_grad,
        norm_grad,
        in_grad,
        conv_grad,
        head_grad,
        gate_grad,
        out_grad_w,
        norm_new,
        in_new,
        conv_new,
        head_new,
        gate_new,
        out_new,
        norm_mom,
        in_mom,
        conv_mom,
        head_mom,
        gate_mom,
        out_mom,
    )


def solution(mesh):
    in_specs = (
        P(("grp", "dp"), None, None),
        P(("grp", "dp"), None),
        P(("grp", "dp"), None, None),
        P("grp"),
        P("grp", None),
        P(None, "grp"),
        P(None, "grp"),
        P("grp"),
        P("grp", None),
        P(None, "grp"),
        P(None, "grp", None),
        P(None, None, "grp"),
        P(None, None, "grp"),
        P(None, "grp"),
        P(None, "grp", None),
    )
    out_specs = (
        P(("grp", "dp"), None, None),
        P(("grp", "dp"), None, None),
        P("grp"),
        P("grp", None),
        P(None, "grp"),
        P(None, "grp"),
        P("grp"),
        P("grp", None),
        P("grp"),
        P("grp", None),
        P(None, "grp"),
        P(None, "grp"),
        P("grp"),
        P("grp", None),
        P(None, "grp"),
        P(None, "grp", None),
        P(None, None, "grp"),
        P(None, None, "grp"),
        P(None, "grp"),
        P(None, "grp", None),
    )
    return jax.shard_map(shards, mesh=mesh, in_specs=in_specs, out_specs=out_specs, check_vma=False)
```

profile of v0, /device:TPU:0, one launch (start us, length us, event | category | flops | bytes accessed | tf_op | source)
XLA Modules:
  0.0 443.5 jit_solution(5044947806766880477)
XLA Ops:
  7.2 3.0 convert_element_type.77
  10.4 0.9 convert_element_type.84
  12.9 8.3 %all-reduce.22 = bf16[768]{0:T(1024)(128)(2,1)S(1)} all-reduce(bf16[768]{0:T(1024)(128)(2,1)S(1)} %dynamic-update-slice), channel_id=1, replica_groups=mesh['grp'=4,'dp'=8] {'grp'}, use_global_device_ids=true, to_apply=%add.22 | all-reduce | flops 768 | bytes 3072
  22.0 5.5 %all-gather = bf16[4,448,5]{1,2,0:T(8,128)(2,1)S(1)} all-gather(bf16[1,448,5]{1,2,0:T(8,128)(2,1)S(1)} %convert_bitcast_fusion.1), channel_id=1, replica_groups=mesh['grp'=4,'dp'=8] {'grp'}, dimensions={0}, use_global_device_ids=true | all-gather | bytes 22400 | tf_op jit(solution)/shard_map/all_gather | solution.py:128
  27.8 5.2 %all-gather.1 = bf16[4,6,3]{1,2,0:T(4,128)(2,1)S(1)} all-gather(bf16[1,6,3]{1,2,0:T(4,128)(2,1)S(1)} %convert_bitcast_fusion.2), channel_id=1, replica_groups=mesh['grp'=4,'dp'=8] {'grp'}, dimensions={0}, use_global_device_ids=true | all-gather | bytes 180 | tf_op jit(solution)/shard_map/all_gather | solution.py:129
  33.2 0.7 fusion.64
  34.0 5.3 %all-gather.2 = bf16[4,1,384]{2,1,0:T(2,128)(2,1)S(1)} all-gather(bf16[1,1,384]{2,1,0:T(2,128)(2,1)S(1)} %reshape.648), channel_id=1, replica_groups=mesh['grp'=4,'dp'=8] {'grp'}, dimensions={0}, use_global_device_ids=true | all-gather | bytes 3840 | tf_op jit(solution)/shard_map/all_gather | solution.py:130
  39.5 14.7 %all-gather.6.cloned.1.call-done = bf16[768,3352]{1,0:T(8,128)(2,1)} async-done(((bf16[192,3352]{1,0:T(8,128)(2,1)}), bf16[768,3352]{1,0:T(8,128)(2,1)}) %all-gather.6.cloned.1.call-update) | async-done | bytes 5148688 | tf_op jit(solution)/shard_map/all_gather | solution.py:127
  54.2 4.8 %convolution_bitcast_fusion = f32[1,256,3352]{1,2,0:T(8,128)S(1)} fusion(bf16[768,3352]{1,0:T(8,128)(2,1)} %all-gather.6.cloned.1.call-done, bf16[1,256,768]{2,1,0:T(8,128)(2,1)} %param.15, f32[768]{0:T(1024)S(1)} %convert_element_type.75, f32[256]{0:T(256)S(1)} %fusion.86), kind=kOutput, calls=%fused_computation.8 | convolution fusion | flops 1318846464 | bytes 8978432 | tf_op jit(solution)/shard_map/dot_general | solution.py:141
  59.5 0.9 copy-done.11
  61.0 3.9 fusion.24
  64.9 1.2 copy-done.3
  66.1 1.2 slice.162
  67.4 0.7 multiply_bitcast_fusion
  69.1 1.4 fusion.67
  70.5 0.7 copy-done.32
  71.2 8.7 %fusion.4 = f32[24,64,256]{2,1,0:T(8,128)S(1)} fusion(f32[256,24,64]{0,2,1:T(8,128)} %bitcast.287, f32[24,256]{1,0:T(8,128)} %get-tuple-element.176, f32[256,256]{1,0:T(8,128)S(1)} %fusion.67, f32[24,256]{1,0:T(8,128)S(1)} %bitcast_add_fusion.4, pred[256,256]{1,0:T(8,128)(4,1)} %fusion.64), kind=kOutput, calls=%fused_computation.7 | convolution fusion | flops 1214251008 | bytes 3522560 | tf_op jit(solution)/shard_map/jvp(vmap(bhts,bshp->bthp))/dot_general | solution.py:44
  79.9 0.6 multiply_reduce_fusion.8
  81.1 1.2 copy-done
  82.2 3.0 fusion.56
  85.5 4.0 fusion.28
  89.6 3.1 multiply_reduce_fusion.7
  92.7 10.4 %fusion.7 = (f32[24,256]{1,0:T(8,128)S(1)}, f32[24,256]{1,0:T(8,128)S(1)}, f32[24,256]{1,0:T(8,128)}, f32[256,256]{1,0:T(8,128)}) fusion(f32[24,256]{1,0:T(8,128)S(1)} %copy-done.48, f32[256,256]{1,0:T(8,128)S(1)} %copy-done.33, f32[24,256]{1,0:T(8,128)S(1)} %bitcast_add_fusion.4, pred[256,256]{1,0:T(8,128)(4,1)S(1)} %copy-done.40, ...), kind=kOutput, calls=%fused_computation.13 | convolution fusion | flops 1228322816 | bytes 3858432 | tf_op jit(solution)/shard_map/transpose(jvp(vmap(bhts,bshp->bthp)))/dot_general | solution.py:44
  103.1 2.5 reduce-window.16
  106.0 1.3 convolution_bitcast_fusion.1
  107.3 1.4 convolution_bitcast_fusion.2
  108.7 1.5 fusion.103
  110.2 7.4 %fusion.2 = f32[24,64,256]{2,1,0:T(8,128)S(1)} fusion(f32[24,64,256]{2,1,0:T(8,128)} %bitcast.285, f32[24,256]{1,0:T(8,128)} %get-tuple-element.176, f32[256,256]{1,0:T(8,128)} %copy-done.32, f32[24,256]{1,0:T(8,128)} %copy-done.49, pred[256,256]{1,0:T(8,128)(4,1)} %fusion.64), kind=kOutput, calls=%fused_computation.6 | convolution fusion | flops 1214251008 | bytes 3522560 | tf_op jit(solution)/shard_map/transpose(jvp(vmap(bhts,bshp->bthp)))/dot_general | solution.py:44
  117.9 1.2 copy-done.12
  119.7 1.2 multiply_reduce_fusion.6
  121.2 0.6 copy-done.10
  121.8 2.0 multiply_reduce_fusion.5
  123.8 0.8 slice_multiply_fusion
  124.6 0.8 slice_multiply_fusion.1
  125.4 0.8 slice_multiply_fusion.2
  126.2 1.7 multiply_reduce_fusion.3
  127.9 1.2 copy-done.18
  129.1 5.8 %fusion.53 = f32[768,3352]{1,0:T(8,128)} fusion(bf16[1,256,768]{2,1,0:T(8,128)(2,1)S(1)} %copy-done.14, f32[768]{0:T(1024)S(1)} %convert_element_type.75, f32[256]{0:T(256)S(1)} %copy-done.46, f32[1,256,1536]{1,2,0:T(8,128)S(1)} %copy-done.24, f32[1,256,1792]{1,2,0:T(8,128)S(1)} %get-tuple-element.177, f32[1,256,24]{1,2,0:T(8,128)S(1)} %get-tuple-element.162), kind=kOutput, calls=%fused_computation.99 | convolution fusion | flops 1321420800 | bytes 14127104 | tf_op jit(solution)/shard_map/td,tk->dk/dot_general | solution.py:157
  135.1 1.3 copy.103
  136.5 84.6 %reduce-scatter.7.cloned.1.call-done = f32[192,3352]{1,0:T(8,128)} async-done(((f32[768,3352]{1,0:T(8,128)}), f32[192,3352]{1,0:T(8,128)}) %reduce-scatter.7.cloned.1.call-update) | async-done | bytes 2574352 | tf_op jit(solution)/shard_map/reduce_scatter | solution.py:164
  225.0 0.6 fusion.106
  225.8 0.7 bitcast_multiply_fusion.2
  227.1 6.5 %fusion.42 = (f32[768]{0:T(1024)}, f32[256]{0:T(256)}, f32[256,768]{1,0:T(8,128)}) fusion(bf16[1,256,768]{2,1,0:T(8,128)(2,1)S(1)} %copy-done.15, f32[256]{0:T(256)} %copy-done.45, f32[768]{0:T(1024)S(1)} %convert_element_type.75, bf16[768,3352]{1,0:T(8,128)(2,1)} %all-gather.6.cloned.1.call-done, f32[1,256,1536]{1,2,0:T(8,128)S(1)} %copy-done.25, ...), kind=kOutput, calls=%fused_computation.88 | convolution fusion | flops 1322009600 | bytes 9768960 | tf_op jit(solution)/shard_map/tk,dk->td/dot_general | solution.py:158
  233.6 11.4 %all-reduce.28 = (f32[768]{0:T(1024)S(1)}, f32[3,24]{1,0:T(4,128)S(1)}, f32[1536]{0:T(1024)S(1)}) all-reduce(f32[768]{0:T(1024)} %get-tuple-element.128, f32[3,24]{1,0:T(4,128)} %pad_add_fusion.1, f32[1536]{0:T(1024)} %get-tuple-element.124), channel_id=2, replica_groups=mesh['grp'=4,'dp'=8] {'grp'}, use_global_device_ids=true, to_apply=%region_13.14.clone | all-reduce | flops 2376 | bytes 19008
  245.2 0.7 multiply_multiply_fusion.12
  245.9 3.4 fusion.32
  249.3 1.0 copy.104
  250.4 39.3 %all-reduce.26 = (f32[192]{0:T(256)S(1)}, f32[5,448]{1,0:T(8,128)S(1)}, f32[3,6]{1,0:T(4,128)S(1)}, f32[384]{0:T(512)S(1)}) all-reduce(f32[192]{0:T(256)S(1)} %dynamic-slice.2, f32[5,448]{1,0:T(8,128)S(1)} %copy.104, f32[3,6]{1,0:T(4,128)S(1)} %constant_dynamic-slice_fusion, ...), channel_id=1, replica_groups=mesh['grp'=4,'dp'=8] {'dp'}, use_global_device_ids=true, to_apply=%region_14.15 | all-reduce | flops 2834 | bytes 22672 | tf_op jit(solution)/shard_map/psum | solution.py:170
  291.5 0.6 multiply_reduce_fusion.11
  292.1 107.2 %all-reduce.31.cloned.1.call-done = (f32[192,3352]{1,0:T(8,128)}, f32[384,768]{1,0:T(8,128)}) async-done(((f32[192,3352]{1,0:T(8,128)}, f32[384,768]{1,0:T(8,128)}), (f32[192,3352]{1,0:T(8,128)}, f32[384,768]{1,0:T(8,128)})) %all-reduce.31.cloned.1.call-update) | async-done | bytes 3754000 | tf_op jit(solution)/shard_map/psum | solution.py:170
  399.3 3.2 multiply_reduce_fusion.2
  402.4 1.0 multiply_reduce_fusion.9
  407.4 2.3 fusion.48
  409.6 6.9 %psum.55 = f32[]{:T(128)} all-reduce(f32[]{:T(128)S(6)} %add.272), channel_id=1, replica_groups=mesh['grp'=4,'dp'=8] {'grp'}, use_global_device_ids=true, to_apply=%region_41.42 | all-reduce | flops 1 | bytes 8 | tf_op jit(solution)/shard_map/psum | solution.py:174
  417.2 5.6 %fusion.51 = (f32[1,192,3352]{2,1,0:T(8,128)S(1)}, f32[1,192,3352]{2,1,0:T(8,128)S(1)}, f32[192,3352]{1,0:T(8,128)}) fusion(f32[192,3352]{1,0:T(8,128)S(1)} %copy-done.6, f32[]{:T(128)S(6)} %min.3, f32[2,192,3352]{2,1,0:T(8,128)} %param.25, f32[192,3352]{1,0:T(8,128)} %param.19), kind=kLoop, calls=%fused_computation.97 | loop fusion | flops 10940928 | bytes 18020356 | tf_op jit(solution)/shard_map/stack | solution.py:96
  423.0 2.0 fusion.65
  425.0 0.6 fusion.78
  425.6 0.6 copy.100
  426.3 0.6 fusion.88
  427.5 0.6 multiply_subtract_fusion.3
  429.3 2.7 pad_maximum_fusion
  432.6 1.6 pad_maximum_fusion.1
  434.2 1.5 copy.155
  435.7 1.0 copy.156
  (244 shorter events, 14.0 us)
Async XLA Ops:
  7.2 3.2 copy-start.26
  7.2 47.0 %all-gather.6.cloned.1.call-start = ((), (), s32[]{:S(2)}) async-start(), calls=%async_computation.3 | async-start | bytes 6635520 | tf_op jit(solution)/shard_map/all_gather | solution.py:127
  10.3 11.0 %copy-start.13 = (bf16[1,256,768]{2,1,0:T(8,128)(2,1)S(1)}, bf16[1,256,768]{2,1,0:T(8,128)(2,1)}, u32[]{:S(2)}) copy-start(bf16[1,256,768]{2,1,0:T(8,128)(2,1)} %param.15) | copy-start | bytes 1179652
  10.3 11.7 %copy-start.37 = (f32[5,448]{1,0:T(8,128)S(1)}, f32[5,448]{1,0:T(8,128)}, u32[]{:S(2)}) copy-start(f32[5,448]{1,0:T(8,128)} %param.20) | copy-start | bytes 26884
  10.3 17.4 %copy-start.59 = (f32[3,6]{1,0:T(4,128)S(1)}, f32[3,6]{1,0:T(4,128)}, u32[]{:S(2)}) copy-start(f32[3,6]{1,0:T(4,128)} %param.21) | copy-start | bytes 220
  10.3 22.9 %copy-start.43 = (s32[1,256]{1,0:T(1,128)S(1)}, s32[1,256]{1,0:T(1,128)}, u32[]{:S(2)}) copy-start(s32[1,256]{1,0:T(1,128)} %param.16) | copy-start | bytes 3076
  10.3 23.6 %copy-start.64 = (f32[384]{0:T(512)S(1)}, f32[384]{0:T(512)}, u32[]{:S(2)}) copy-start(f32[384]{0:T(512)} %param.22) | copy-start | bytes 4612
  10.4 75.1 %all-gather.8.cloned.1.call-start = ((), (), s32[]{:S(2)}) async-start(), calls=%async_computation.4 | async-start | bytes 2949120 | tf_op jit(solution)/shard_map/all_gather | solution.py:131
  11.3 125.1 %reduce-scatter.9.cloned.1.call-start = ((), (), s32[]{:S(2)}) async-start(), calls=%async_computation.6 | async-start | bytes 5898240 | tf_op jit(solution)/shard_map/reduce_scatter | solution.py:168
  22.0 37.1 %copy-start.45 = (f32[256]{0:T(256)}, f32[256]{0:T(256)S(1)}, u32[]{:S(2)}) copy-start(f32[256]{0:T(256)S(1)} %fusion.86) | copy-start | bytes 3076
  27.7 31.8 %copy-start.35 = (f32[1792]{0:T(1024)}, f32[1792]{0:T(1024)S(1)}, u32[]{:S(2)}) copy-start(f32[1792]{0:T(1024)S(1)} %get-tuple-element.133) | copy-start | bytes 21508
  33.1 34.3 %copy-start.69 = (f32[24]{0:T(128)}, f32[24]{0:T(128)S(1)}, u32[]{:S(2)}) copy-start(f32[24]{0:T(128)S(1)} %get-tuple-element.192) | copy-start | bytes 292
  33.1 34.3 %copy-start.70 = (f32[24]{0:T(128)}, f32[24]{0:T(128)S(1)}, u32[]{:S(2)}) copy-start(f32[24]{0:T(128)S(1)} %get-tuple-element.194) | copy-start | bytes 292
  39.4 20.1 %copy-start.51 = (f32[1,256]{1,0:T(1,128)}, f32[1,256]{1,0:T(1,128)S(1)}, u32[]{:S(2)}) copy-start(f32[1,256]{1,0:T(1,128)S(1)} %get-tuple-element.195) | copy-start | bytes 3076
  39.5 20.1 %copy-start.53 = (f32[1,256]{1,0:T(1,128)}, f32[1,256]{1,0:T(1,128)S(1)}, u32[]{:S(2)}) copy-start(f32[1,256]{1,0:T(1,128)S(1)} %get-tuple-element.196) | copy-start | bytes 3076
  39.5 20.1 %copy-start.55 = (f32[1,256]{1,0:T(1,128)}, f32[1,256]{1,0:T(1,128)S(1)}, u32[]{:S(2)}) copy-start(f32[1,256]{1,0:T(1,128)S(1)} %get-tuple-element.197) | copy-start | bytes 3076
  59.5 5.4 %copy-start.9 = (f32[1,255,1792]{1,2,0:T(8,128)}, f32[1,255,1792]{1,2,0:T(8,128)S(1)}, u32[]{:S(2)}) copy-start(f32[1,255,1792]{1,2,0:T(8,128)S(1)} %slice.157) | copy-start | bytes 5483524
  69.1 23.6 %copy-start.49 = (f32[24,256]{1,0:T(8,128)}, f32[24,256]{1,0:T(8,128)S(1)}, u32[]{:S(2)}) copy-start(f32[24,256]{1,0:T(8,128)S(1)} %bitcast_add_fusion.4) | copy-start | bytes 73732
  71.2 8.7 %copy-start.4 = (f32[1,256,1792]{1,2,0:T(8,128)S(1)}, f32[1,256,1792]{1,2,0:T(8,128)}, u32[]{:S(2)}) copy-start(f32[1,256,1792]{1,2,0:T(8,128)} %copy-done.3) | copy-start | bytes 5505028
  85.3 135.8 %reduce-scatter.7.cloned.1.call-start = ((), (), s32[]{:S(2)}) async-start(), calls=%async_computation.5 | async-start | bytes 13271040 | tf_op jit(solution)/shard_map/reduce_scatter | solution.py:164
  85.5 4.0 copy-start.1
  85.5 4.0 copy-start.5
  85.5 4.0 copy-start.23
  89.5 3.1 copy-start.31
  89.5 3.1 copy-start.33
  89.6 3.1 copy-start.40
  89.6 3.1 copy-start.48
  92.7 10.4 %copy-start.20 = (f32[1,256,1536]{1,2,0:T(8,128)}, f32[1,256,1536]{1,2,0:T(8,128)S(1)}, u32[]{:S(2)}) copy-start(f32[1,256,1536]{1,2,0:T(8,128)S(1)} %get-tuple-element.160) | copy-start | bytes 4718596
  110.2 17.7 %copy-start.34 = (f32[1,256,24]{1,2,0:T(8,128)}, f32[1,256,24]{1,2,0:T(8,128)S(1)}, u32[]{:S(2)}) copy-start(f32[1,256,24]{1,2,0:T(8,128)S(1)} %get-tuple-element.162) | copy-start | bytes 73732
  110.2 7.4 %copy-start.21 = (f32[1,256,1536]{1,2,0:T(8,128)S(1)}, f32[1,256,1536]{1,2,0:T(8,128)}, u32[]{:S(2)}) copy-start(f32[1,256,1536]{1,2,0:T(8,128)} %copy-done.20) | copy-start | bytes 4718596
  126.1 3.0 copy-start.14
  126.2 3.0 copy-start.24
  126.2 3.0 copy-start.46
  134.9 114.4 %reduce-scatter.11.cloned.1.call-start = ((), (), s32[]{:S(2)}) async-start(), calls=%async_computation.7 | async-start | bytes 1146880
  136.4 262.9 %all-reduce.31.cloned.1.call-start = ((), (), s32[]{:S(2)}) async-start(), calls=%async_computation.8 | async-start | bytes 7667712 | tf_op jit(solution)/shard_map/psum | solution.py:170
  221.1 2.8 copy-start.77
  221.1 3.3 copy-start.74
  221.1 3.9 copy-start.50
  221.1 4.5 %copy-start.44 = (f32[1536]{0:T(1024)S(1)}, f32[1536]{0:T(1024)}, u32[]{:S(2)}) copy-start(f32[1536]{0:T(1024)} %get-tuple-element.159) | copy-start | bytes 18436
  221.1 4.7 %copy-start.81 = (f32[24]{0:T(128)S(1)}, f32[24]{0:T(128)}, u32[]{:S(2)}) copy-start(f32[24]{0:T(128)} %get-tuple-element.174) | copy-start | bytes 292
  221.1 5.4 %copy-start.75 = (f32[24]{0:T(128)S(1)}, f32[24]{0:T(128)}, u32[]{:S(2)}) copy-start(f32[24]{0:T(128)} %get-tuple-element.161) | copy-start | bytes 292
  221.1 6.0 %copy-start.15 = (bf16[1,256,768]{2,1,0:T(8,128)(2,1)S(1)}, bf16[1,256,768]{2,1,0:T(8,128)(2,1)}, u32[]{:S(2)}) copy-start(bf16[1,256,768]{2,1,0:T(8,128)(2,1)} %param.15) | copy-start | bytes 1179652
  221.1 6.0 %copy-start.25 = (f32[1,256,1536]{1,2,0:T(8,128)S(1)}, f32[1,256,1536]{1,2,0:T(8,128)}, u32[]{:S(2)}) copy-start(f32[1,256,1536]{1,2,0:T(8,128)} %get-tuple-element.167) | copy-start | bytes 4718596
  227.1 18.8 %copy-start.2 = (f32[1,256,1536]{1,2,0:T(8,128)S(1)}, f32[1,256,1536]{1,2,0:T(8,128)}, u32[]{:S(2)}) copy-start(f32[1,256,1536]{1,2,0:T(8,128)} %copy-done) | copy-start | bytes 4718596
  289.6 135.3 %copy-start.39 = (f32[5,448]{1,0:T(8,128)}, f32[5,448]{1,0:T(8,128)S(1)}, u32[]{:S(2)}) copy-start(f32[5,448]{1,0:T(8,128)S(1)} %get-tuple-element.206) | copy-start | bytes 26884
  289.7 136.6 %copy-start.58 = (f32[3,6]{1,0:T(4,128)}, f32[3,6]{1,0:T(4,128)S(1)}, u32[]{:S(2)}) copy-start(f32[3,6]{1,0:T(4,128)S(1)} %get-tuple-element.207) | copy-start | bytes 220
  289.7 137.8 %copy-start.63 = (f32[384]{0:T(512)}, f32[384]{0:T(512)S(1)}, u32[]{:S(2)}) copy-start(f32[384]{0:T(512)S(1)} %get-tuple-element.208) | copy-start | bytes 4612
  289.7 138.4 %copy-start.80 = (f32[192]{0:T(256)}, f32[192]{0:T(256)S(1)}, u32[]{:S(2)}) copy-start(f32[192]{0:T(256)S(1)} %get-tuple-element.204) | copy-start | bytes 2308
  399.3 3.2 copy-start.16
  399.3 8.1 %copy-start.29 = (bf16[1,256,768]{2,1,0:T(8,128)(2,1)S(1)}, bf16[1,256,768]{2,1,0:T(8,128)(2,1)}, u32[]{:S(2)}) copy-start(bf16[1,256,768]{2,1,0:T(8,128)(2,1)} %param.17) | copy-start | bytes 1179652
  399.3 8.1 %copy-start.47 = (f32[256]{0:T(256)S(1)}, f32[256]{0:T(256)}, u32[]{:S(2)}) copy-start(f32[256]{0:T(256)} %copy-done.45) | copy-start | bytes 3076
  402.4 14.8 %copy-start.6 = (f32[192,3352]{1,0:T(8,128)S(1)}, f32[192,3352]{1,0:T(8,128)}, u32[]{:S(2)}) copy-start(f32[192,3352]{1,0:T(8,128)} %get-tuple-element.205) | copy-start | bytes 7723012
  417.2 5.6 %copy-start.17 = (f32[384,768]{1,0:T(8,128)S(1)}, f32[384,768]{1,0:T(8,128)}, u32[]{:S(2)}) copy-start(f32[384,768]{1,0:T(8,128)} %get-tuple-element.209) | copy-start | bytes 3538948
  417.2 5.6 %copy-start.27 = (f32[384,768]{1,0:T(8,128)S(1)}, f32[384,768]{1,0:T(8,128)}, u32[]{:S(2)}) copy-start(f32[384,768]{1,0:T(8,128)} %param.23) | copy-start | bytes 3538948
  417.2 5.6 %copy-start.30 = (f32[2,384,768]{2,1,0:T(8,128)S(1)}, f32[2,384,768]{2,1,0:T(8,128)}, u32[]{:S(2)}) copy-start(f32[2,384,768]{2,1,0:T(8,128)} %param.29) | copy-start | bytes 7077892
  422.9 3.4 copy-start.60
  422.9 3.4 copy-start.67
  422.9 3.4 copy-start.68
  422.9 4.6 %copy-start.61 = (f32[384]{0:T(512)S(1)}, f32[384]{0:T(512)}, u32[]{:S(2)}) copy-start(f32[384]{0:T(512)} %get-tuple-element.135) | copy-start | bytes 4612
  422.9 4.5 %copy-start.62 = (f32[384]{0:T(512)S(1)}, f32[384]{0:T(512)}, u32[]{:S(2)}) copy-start(f32[384]{0:T(512)} %get-tuple-element.136) | copy-start | bytes 4612
  423.0 4.5 %copy-start.65 = (f32[384]{0:T(512)S(1)}, f32[384]{0:T(512)}, u32[]{:S(2)}) copy-start(f32[384]{0:T(512)} %param.22) | copy-start | bytes 4612
  423.0 5.1 %copy-start.71 = (f32[1,192]{1,0:T(1,128)S(1)}, f32[1,192]{1,0:T(1,128)}, u32[]{:S(2)}) copy-start(f32[1,192]{1,0:T(1,128)} %get-tuple-element.190) | copy-start | bytes 2308
  423.0 5.1 %copy-start.72 = (f32[1,192]{1,0:T(1,128)S(1)}, f32[1,192]{1,0:T(1,128)}, u32[]{:S(2)}) copy-start(f32[1,192]{1,0:T(1,128)} %get-tuple-element.191) | copy-start | bytes 2308
  423.0 5.1 %copy-start.79 = (f32[192]{0:T(256)S(1)}, f32[192]{0:T(256)}, u32[]{:S(2)}) copy-start(f32[192]{0:T(256)} %param.18) | copy-start | bytes 2308
  (24 other events, 38.5 us)
Sparse Core Ops, SparseCore 0:
  10.4 43.7 all-gather.5
  56.3 24.0 all-gather.7
  85.4 47.9 reduce-scatter.8
  135.8 85.1 reduce-scatter.6
  224.1 24.0 reduce-scatter.10
  251.7 147.5 all-reduce.30
where the time goes:
time: 444 us
  waiting for transfers between devices  207 us (47%)
  blocking collectives  81.9 us (18%)
  matrix products  58 us (13%)
  other arithmetic  53.6 us (12%)
  between operations  22.5 us (5%)
  local copies, waits for them, and re-layouts  20.5 us (5%)
    psum x1, waiting for transfers between devices, shards(): lax.psum((all_owned[0], all_owned[1], all_owned[2], all_owned[3], all_own...  107 us
    reduce_scatter x1, waiting for transfers between devices, shards(): lax.psum_scatter(grad_in_w, 'grp', scatter_dimension=0, tiled=True)  84.6 us
    psum x1, blocking collectives, shards(): lax.psum((all_owned[0], all_owned[1], all_owned[2], all_owned[3], all_own...  39.3 us
    dot_general x3, matrix products, scan_blocks(): jnp.einsum('bhts,bshp->bthp', weighted, block_vals, precision=highest)  26.5 us
    unnamed x2, blocking collectives  19.7 us
    unnamed x177, local copies, waits for them, and re-layouts  17 us
    all_gather x1, waiting for transfers between devices, shards(): lax.all_gather(in_weight.astype(half), 'grp', axis=0, tiled=True)  14.7 us
    another operation x10, other arithmetic, adam_update(): return (updated, jnp.stack([first, second_root]))  14.3 us
  transfers between devices with their start and end apart: 6, of which 3 were waited for; matrix products, arithmetic and copies ran while one was open for 21% of the time, Pallas kernels for 0%

commit v1 on v0

--- a/solution.py
+++ b/solution.py
@@ -1,6 +1,8 @@
 import jax
 import jax.numpy as jnp
 from jax import lax
+from jax.experimental import pallas as pl
+from jax.experimental.pallas import tpu as pltpu
 from jax.sharding import PartitionSpec as P
 
 STRETCH = 256
@@ -103,6 +105,218 @@
     return total
 
 
+MESH = pl.DeviceIdType.MESH
+BITS = 3
+SLAB = 16
+
+
+def chunks_of(shapes):
+    found = []
+    for which, (_, cols) in enumerate(shapes):
+        width = 768 if which == 0 else 384
+        start = 0
+        while start < cols:
+            found.append((which, start, min(width, cols - start)))
+            start += width
+    order = sorted(found, key=lambda item: -item[2] * shapes[item[0]][0])
+    return tuple(order)
+
+
+def reduce_body(shapes, plan, *refs):
+    count = len(shapes)
+    grads = refs[:count]
+    finals = refs[count : 2 * count]
+    scratch = refs[2 * count : 2 * count + 6 * count]
+    pair_in, half_out, half_in, first_in, second_in, third_in = [
+        scratch[k * count : (k + 1) * count] for k in range(6)
+    ]
+    send_sem, recv_sem = refs[-2:]
+    grp, dp = lax.axis_index("grp"), lax.axis_index("dp")
+    core, cross = lax.rem(grp, 2), lax.div(grp, 2)
+    other_core, other_cross = 1 - core, 1 - cross
+    bit_vals = [lax.rem(lax.div(dp, 1 << k), 2) for k in range(BITS)]
+    core_dev = {"grp": cross * 2 + other_core, "dp": dp}
+    cross_dev = {"grp": other_cross * 2 + core, "dp": dp}
+    dp_devs = [
+        {"grp": grp, "dp": dp + (1 - 2 * bit_vals[k]) * (1 << k)} for k in range(BITS)
+    ]
+    barrier = pltpu.get_barrier_semaphore()
+    for device in [core_dev, cross_dev] + dp_devs:
+        pl.semaphore_signal(barrier, inc=1, device_id=device, device_id_type=MESH)
+    pl.semaphore_wait(barrier, 2 + BITS)
+
+    def span(start, rows):
+        return pl.ds(pl.multiple_of(start, 8), rows)
+
+    def remote(src, dst, chunk, slot, device):
+        copy = pltpu.make_async_remote_copy(
+            src_ref=src,
+            dst_ref=dst,
+            send_sem=send_sem.at[chunk, slot],
+            recv_sem=recv_sem.at[chunk, slot],
+            device_id=device,
+            device_id_type=MESH,
+        )
+        copy.start()
+        return copy
+
+    copies = {}
+    for chunk, (which, start, width) in enumerate(plan):
+        rows = shapes[which][0] // 4
+        cols = slice(start, start + width)
+        for keep in range(2):
+            origin = (2 * keep + other_core) * rows
+            copies[chunk, keep] = remote(
+                grads[which].at[span(origin, rows), cols],
+                pair_in[which].at[keep, :, cols],
+                chunk,
+                keep,
+                core_dev,
+            )
+
+    def tiles(rows, step):
+        height = SLAB if rows % SLAB == 0 else 8
+
+        @pl.loop(0, rows // height)
+        def _(index):
+            step(index * height, height)
+
+    def offset_to(which, levels):
+        rows = shapes[which][0] // 4
+        total = 0
+        for k in range(levels):
+            total = total + bit_vals[k] * (rows >> (k + 1))
+        return total
+
+    def stage(chunk, number):
+        which, start, width = plan[chunk]
+        rows = shapes[which][0] // 4
+        cols = slice(start, start + width)
+        grad, final = grads[which], finals[which]
+        pair, out_half, in_half = pair_in[which], half_out[which], half_in[which]
+        level_in = [first_in[which], second_in[which], third_in[which]]
+        if number == 0:
+            copies[chunk, 0].wait_recv()
+            copies[chunk, 1].wait_recv()
+
+            def send_part(base, height):
+                own = grad[span((2 * other_cross + core) * rows + base, height), cols]
+                got = pair[other_cross, span(base, height), cols]
+                out_half[span(base, height), cols] = (own + got).astype(out_half.dtype)
+
+            tiles(rows, send_part)
+            copies[chunk, 2] = remote(
+                out_half.at[:, cols], in_half.at[:, cols], chunk, 2, cross_dev
+            )
+
+            def keep_part(base, height):
+                own = grad[span((2 * cross + core) * rows + base, height), cols]
+                pair[cross, span(base, height), cols] += own
+
+            tiles(rows, keep_part)
+        elif number == 1:
+            copies[chunk, 2].wait_recv()
+            half = rows // 2
+
+            def add_cross(base, height):
+                got = in_half[span(base, height), cols].astype(jnp.float32)
+                pair[cross, span(base, height), cols] += got
+
+            tiles(rows, add_cross)
+            copies[chunk, 3] = remote(
+                pair.at[cross, span((1 - bit_vals[0]) * half, half), cols],
+                level_in[0].at[:, cols],
+                chunk,
+                3,
+                dp_devs[0],
+            )
+        elif number < 1 + BITS:
+            level = number - 2
+            size = rows >> (level + 1)
+            copies[chunk, 3 + level].wait_recv()
+            target = level_in[level]
+
+            def add_level(base, height):
+                if level == 0:
+                    own = pair[cross, span(bit_vals[0] * size + base, height), cols]
+                else:
+                    own = level_in[level - 1][span(bit_vals[level] * size + base, height), cols]
+                target[span(base, height), cols] += own
+
+            tiles(size, add_level)
+            half = size // 2
+            copies[chunk, 4 + level] = remote(
+                target.at[span((1 - bit_vals[level + 1]) * half, half), cols],
+                level_in[level + 1].at[:, cols],
+                chunk,
+                4 + level,
+                dp_devs[level + 1],
+            )
+        elif number == 1 + BITS:
+            level = BITS - 1
+            size = rows >> BITS
+            copies[chunk, 3 + level].wait_recv()
+            place = offset_to(which, BITS)
+
+            def add_last(base, height):
+                own = level_in[level - 1][span(bit_vals[level] * size + base, height), cols]
+                got = level_in[level][span(base, height), cols]
+                final[span(place + base, height), cols] = own + got
+
+            tiles(size, add_last)
+            gather(chunk, 0)
+        else:
+            done = number - 2 - BITS
+            copies[chunk, 3 + BITS + done].wait_recv()
+            if done < BITS - 1:
+                gather(chunk, done + 1)
+
+    def gather(chunk, number):
+        which, start, width = plan[chunk]
+        rows = shapes[which][0] // 4
+        levels = BITS - number
+        size = rows >> levels
+        piece = finals[which].at[span(offset_to(which, levels), size), start : start + width]
+        copies[chunk, 3 + BITS + number] = remote(
+            piece, piece, chunk, 3 + BITS + number, dp_devs[levels - 1]
+        )
+
+    stages = 2 + 2 * BITS
+    for tick in range(len(plan) + stages - 1):
+        for number in reversed(range(stages)):
+            chunk = tick - number
+            if 0 <= chunk < len(plan):
+                stage(chunk, number)
+    for copy in copies.values():
+        copy.wait_send()
+
+
+def reduce_grads(arrays):
+    shapes = tuple(array.shape for array in arrays)
+    plan = chunks_of(shapes)
+    wide = jnp.float32
+    kinds = (jnp.bfloat16, jnp.bfloat16, jnp.float32)
+    quarter = [(rows // 4, cols) for rows, cols in shapes]
+    scratch = [pltpu.VMEM((2,) + size, wide) for size in quarter]
+    scratch += [pltpu.VMEM(size, kind) for size, kind in zip(quarter, kinds)]
+    scratch += [pltpu.VMEM(size, kind) for size, kind in zip(quarter, kinds)]
+    for level in range(BITS):
+        scratch += [pltpu.VMEM((rows >> (level + 1), cols), wide) for rows, cols in quarter]
+    slots = 3 + 2 * BITS
+    scratch += [pltpu.SemaphoreType.DMA((len(plan), slots))] * 2
+    return pl.pallas_call(
+        lambda *refs: reduce_body(shapes, plan, *refs),
+        out_shape=[jax.ShapeDtypeStruct(size, wide) for size in quarter],
+        in_specs=[pl.BlockSpec(memory_space=pltpu.VMEM)] * len(shapes),
+        out_specs=[pl.BlockSpec(memory_space=pltpu.VMEM)] * len(shapes),
+        scratch_shapes=scratch,
+        compiler_params=pltpu.CompilerParams(
+            collective_id=0, has_side_effects=True, vmem_limit_bytes=58 * 1024 * 1024
+        ),
+        name="reduce_grads",
+    )(*arrays)
+
+
 def shards(
     inputs,
     segment_ids,
@@ -154,22 +368,51 @@
     d_mixed = jnp.einsum("td,id->ti", cotangent, out_half, preferred_element_type=wide)
     d_proj, grad_conv, grad_head, grad_gate = mixer_back(d_mixed.reshape(seq_count, length, -1))
     dproj_half = d_proj.reshape(row_count, -1).astype(half)
-    grad_in_w = jnp.einsum("td,tk->dk", normed, dproj_half, preferred_element_type=wide)
+    main_cols = dproj_half.shape[1] // 128 * 128
+    grad_main = jnp.einsum(
+        "td,tk->dk", normed, dproj_half[:, :main_cols], preferred_element_type=wide
+    )
+    grad_tail = jnp.einsum(
+        "td,tk->dk", normed, dproj_half[:, main_cols:], preferred_element_type=wide
+    )
     d_normed = jnp.einsum("tk,dk->td", dproj_half, in_half, preferred_element_type=wide)
     norm_back = jax.vjp(norm_rows, input_wide, norm_wide)[1]
     d_input, grad_norm = norm_back(d_normed)
     input_grad = (cotangent.astype(wide) + d_input).reshape(seq_count, length, width)
-    all_owned = (
-        lax.psum_scatter(grad_norm, "grp", scatter_dimension=0, tiled=True),
-        lax.psum_scatter(grad_in_w, "grp", scatter_dimension=0, tiled=True),
-        lax.psum_scatter(grad_conv, "grp", scatter_dimension=1, tiled=True),
-        lax.psum_scatter(grad_head, "grp", scatter_dimension=1, tiled=True),
-        lax.psum_scatter(grad_gate, "grp", scatter_dimension=0, tiled=True),
-        lax.psum_scatter(out_w_local, "grp", scatter_dimension=0, tiled=True),
-    )
-    norm_grad, in_grad, conv_grad, head_grad, gate_grad, out_grad_w = lax.psum(
-        (all_owned[0], all_owned[1], all_owned[2], all_owned[3], all_owned[4], all_owned[5]), "dp"
-    )
+    grp_size = 4
+    own_rows = width // grp_size
+    conv_cols = grad_conv.shape[1] // grp_size
+    head_cols = grad_head.shape[1] // grp_size
+    gate_size = grad_gate.shape[0] // grp_size
+    small = [
+        grad_norm.reshape(grp_size, -1),
+        grad_gate.reshape(grp_size, -1),
+        jnp.transpose(grad_conv.reshape(-1, grp_size, conv_cols), (1, 0, 2)).reshape(grp_size, -1),
+        jnp.transpose(grad_head.reshape(-1, grp_size, head_cols), (1, 0, 2)).reshape(grp_size, -1),
+    ]
+    small = jnp.concatenate(small, axis=1)
+    small_size = small.shape[1]
+    tail_cols = grad_tail.shape[1]
+    spare = 128 - tail_cols
+    small = jnp.pad(small, ((0, 0), (0, own_rows * spare - small_size)))
+    small = small.reshape(grp_size * own_rows, spare)
+    grad_last = jnp.concatenate([grad_tail, small], axis=1)
+    reduced = reduce_grads((grad_main, out_w_local, grad_last))
+    groups = lax.axis_size("dp")
+    step = 1 << BITS
+    while step < groups:
+        pairs = [(index, index ^ step) for index in range(groups)]
+        reduced = [piece + lax.ppermute(piece, "dp", pairs) for piece in reduced]
+        step *= 2
+    main_sum, out_grad_w, last_sum = reduced
+    in_grad = jnp.concatenate([main_sum, last_sum[:, :tail_cols]], axis=1)
+    flat = last_sum[:, tail_cols:].reshape(-1)
+    norm_grad = flat[:own_rows]
+    gate_grad = flat[own_rows : own_rows + gate_size]
+    conv_at = own_rows + gate_size
+    head_at = conv_at + grad_conv.shape[0] * conv_cols
+    conv_grad = flat[conv_at:head_at].reshape(-1, conv_cols)
+    head_grad = flat[head_at:small_size].reshape(-1, head_cols)
     local_squares = square_sum((norm_grad, in_grad, conv_grad, head_grad, gate_grad, out_grad_w))
     squares = lax.psum(local_squares, "grp")
     clip_factor = jnp.minimum(1.0, clip_limit / jnp.sqrt(squares + 1e-06))

time: 444 us -> 336 us (0.76); the launches traced: 444 us -> 330 us
  waiting for transfers between devices: 207 us -> 12.6 us
  Pallas kernels: 0 us -> 120 us
  blocking collectives: 81.9 us -> 30.8 us
  other arithmetic: 53.6 us -> 74.6 us
  matrix products: 58 us -> 48.3 us
    pallas_call x0 -> x1, Pallas kernels: none -> 120 us  [reduce_grads(): pl.pallas_call(lambda *refs: reduce_body(shapes, plan, *refs), out_shape=...]
    psum x1 -> x0, waiting for transfers between devices: 107 us -> none  [shards(): lax.psum((all_owned[0], all_owned[1], all_owned[2], all_owned[3], all_own...]
    reduce_scatter x2 -> x0, waiting for transfers between devices: 84.6 us -> none  [the longest x1 84.6 us: shards(): lax.psum_scatter(grad_in_w, 'grp', scatter_dimension=0, tiled=True)]
    psum x1 -> x0, blocking collectives: 39.3 us -> none  [shards(): lax.psum((all_owned[0], all_owned[1], all_owned[2], all_owned[3], all_own...]
    unnamed x2 -> x1, blocking collectives: 19.7 us -> 8.34 us
    sub x2 -> x5, other arithmetic: 1.2 us -> 10.2 us  [adam_update(): master - learn_rate * (first_hat / (root_hat + adam_eps) + weight_decay *...]
    unnamed x177 -> x153, local copies, waits for them, and re-layouts: 17 us -> 12 us
    another operation x10 -> x7, other arithmetic: 14.3 us -> 9.54 us  [adam_update(): return (updated, jnp.stack([first, second_root]))]
  transfers between devices with their start and end apart: 6 -> 2, of which waited for: 3 -> 1; matrix products, arithmetic and copies ran while one was open for 21% -> 9% of each run, Pallas kernels for 0% -> 0%
where the time goes in v1:
time: 336 us; the launch traced here: 330 us
  Pallas kernels  120 us (36%)
  other arithmetic  74.6 us (22%)
  matrix products  48.3 us (14%)
  blocking collectives  30.8 us (9%)
  local copies, waits for them, and re-layouts  23.8 us (7%)
  between operations  20.5 us (6%)
  waiting for transfers between devices  12.6 us (4%)
    pallas_call x1, Pallas kernels, reduce_grads(): pl.pallas_call(lambda *refs: reduce_body(shapes, plan, *refs), out_shape=...  120 us
    dot_general x3, matrix products, scan_blocks(): jnp.einsum('bhts,bshp->bthp', weighted, block_vals, precision=highest)  24.7 us
    all_gather x1, waiting for transfers between devices, shards(): lax.all_gather(in_weight.astype(half), 'grp', axis=0, tiled=True)  12.5 us
    unnamed x153, local copies, waits for them, and re-layouts  12 us
    reduce_sum x6, other arithmetic, square_sum(): total = total + jnp.sum(grad_arr * grad_arr)  10.4 us
    sub x5, other arithmetic, adam_update(): master - learn_rate * (first_hat / (root_hat + adam_eps) + weight_decay *...  10.2 us
    another operation x7, other arithmetic, adam_update(): return (updated, jnp.stack([first, second_root]))  9.54 us
    unnamed x1, blocking collectives  8.34 us
  transfers between devices with their start and end apart: 2, of which 1 were waited for; matrix products, arithmetic and copies ran while one was open for 9% of the time, Pallas kernels for 0%

profile of v1, /device:TPU:0, one launch (start us, length us, event | category | flops | bytes accessed | tf_op | source)
XLA Modules:
  0.0 330.2 jit_solution(9204958554468331792)
XLA Ops:
  7.2 3.0 convert_element_type.70
  10.5 0.9 convert_element_type.77
  12.9 8.3 %all-reduce.23 = bf16[768]{0:T(1024)(128)(2,1)S(1)} all-reduce(bf16[768]{0:T(1024)(128)(2,1)S(1)} %dynamic-update-slice), channel_id=1, replica_groups=mesh['grp'=4,'dp'=8] {'grp'}, use_global_device_ids=true, to_apply=%add.23 | all-reduce | flops 768 | bytes 3072
  22.0 5.5 %all-gather = bf16[4,448,5]{1,2,0:T(8,128)(2,1)S(1)} all-gather(bf16[1,448,5]{1,2,0:T(8,128)(2,1)S(1)} %convert_bitcast_fusion), channel_id=1, replica_groups=mesh['grp'=4,'dp'=8] {'grp'}, dimensions={0}, use_global_device_ids=true | all-gather | bytes 22400 | tf_op jit(solution)/shard_map/all_gather | solution.py:342
  27.6 5.2 %all-gather.1 = bf16[4,6,3]{1,2,0:T(4,128)(2,1)S(1)} all-gather(bf16[1,6,3]{1,2,0:T(4,128)(2,1)S(1)} %convert_bitcast_fusion.1), channel_id=1, replica_groups=mesh['grp'=4,'dp'=8] {'grp'}, dimensions={0}, use_global_device_ids=true | all-gather | bytes 180 | tf_op jit(solution)/shard_map/all_gather | solution.py:343
  33.6 5.3 %all-gather.2 = bf16[4,1,384]{2,1,0:T(2,128)(2,1)S(1)} all-gather(bf16[1,1,384]{2,1,0:T(2,128)(2,1)S(1)} %reshape.772), channel_id=1, replica_groups=mesh['grp'=4,'dp'=8] {'grp'}, dimensions={0}, use_global_device_ids=true | all-gather | bytes 3840 | tf_op jit(solution)/shard_map/all_gather | solution.py:344
  41.0 0.7 fusion.58
  41.7 12.5 %all-gather.6.cloned.1.call-done = bf16[768,3352]{1,0:T(8,128)(2,1)} async-done(((bf16[192,3352]{1,0:T(8,128)(2,1)}), bf16[768,3352]{1,0:T(8,128)(2,1)}) %all-gather.6.cloned.1.call-update) | async-done | bytes 5148688 | tf_op jit(solution)/shard_map/all_gather | solution.py:341
  54.2 4.8 %convolution_bitcast_fusion = f32[1,256,3352]{1,2,0:T(8,128)S(1)} fusion(bf16[768,3352]{1,0:T(8,128)(2,1)} %all-gather.6.cloned.1.call-done, bf16[1,256,768]{2,1,0:T(8,128)(2,1)} %param.15, f32[768]{0:T(1024)S(1)} %convert_element_type.68, f32[256]{0:T(256)S(1)} %fusion.93), kind=kOutput, calls=%fused_computation.8 | convolution fusion | flops 1318846464 | bytes 8978432 | tf_op jit(solution)/shard_map/dot_general | solution.py:355
  59.5 0.9 copy-done.10
  61.0 4.4 %fusion.31 = (f32[1,256,1792]{1,2,0:T(8,128)S(1)}, f32[1,256,1792]{1,2,0:T(8,128)}) fusion(f32[256]{0:T(256)S(1)} %bitcast.293, f32[1,253,1792]{1,2,0:T(8,128)S(1)} %slice.193, f32[1792]{0:T(1024)S(1)} %get-tuple-element.137, f32[256]{0:T(256)S(1)} %bitcast.291, f32[1,254,1792]{1,2,0:T(8,128)S(1)} %slice.191, f32[1792]{0:T(1024)S(1)} %get-tuple-element.138, ...), kind=kLoop, calls=%fused_computation.60 | loop fusion | flops 6881280 | bytes 11005952 | tf_op jit(solution)/shard_map/jvp(vmap(jit(silu)))/mul | solution.py:77
  65.4 1.2 copy-done.2
  66.7 1.2 slice.194
  67.9 0.7 multiply_bitcast_fusion
  69.6 1.4 fusion.61
  71.0 0.7 copy-done.30
  71.7 8.7 %fusion.4 = f32[24,64,256]{2,1,0:T(8,128)S(1)} fusion(f32[256,24,64]{0,2,1:T(8,128)} %bitcast.277, f32[24,256]{1,0:T(8,128)} %get-tuple-element.178, f32[256,256]{1,0:T(8,128)S(1)} %fusion.61, f32[24,256]{1,0:T(8,128)S(1)} %bitcast_add_fusion.4, pred[256,256]{1,0:T(8,128)(4,1)} %fusion.58), kind=kOutput, calls=%fused_computation.7 | convolution fusion | flops 1214251008 | bytes 3522560 | tf_op jit(solution)/shard_map/jvp(vmap(bhts,bshp->bthp))/dot_general | solution.py:46
  80.5 1.8 multiply_reduce_fusion.8
  82.3 3.3 %fusion.37 = (f32[1536]{0:T(1024)S(1)}, f32[256]{0:T(256)S(1)}, f32[256,1536]{0,1:T(8,128)S(1)}) fusion(f32[1,256,1536]{1,2,0:T(8,128)} %get-tuple-element.167, f32[256]{0:T(256)S(1)} %fusion.94, f32[1536]{0:T(1024)S(1)} %reshape.774, bf16[1536,768]{1,0:T(8,128)(2,1)} %all-gather.8.cloned.1.call-done, bf16[1,256,768]{2,1,0:T(8,128)(2,1)} %param.17), kind=kOutput, calls=%fused_computation.72 | convolution fusion | flops 606337280 | bytes 5912576 | tf_op jit(solution)/shard_map/td,id->ti/dot_general | solution.py:368
  86.0 3.2 multiply_reduce_fusion.7
  89.2 5.5 %fusion.2 = f32[24,64,256]{2,1,0:T(8,128)S(1)} fusion(f32[24,64,256]{2,1,0:T(8,128)S(1)} %bitcast.273, f32[24,256]{1,0:T(8,128)S(1)} %copy-done.41, f32[256,256]{1,0:T(8,128)S(1)} %copy-done.31, f32[24,256]{1,0:T(8,128)S(1)} %copy-done.43, pred[256,256]{1,0:T(8,128)(4,1)S(1)} %copy-done.33), kind=kOutput, calls=%fused_computation.6 | convolution fusion | flops 1214251008 | bytes 3522560 | tf_op jit(solution)/shard_map/transpose(jvp(vmap(bhts,bshp->bthp)))/dot_general | solution.py:46
  94.7 10.5 %fusion.7 = (f32[24,256]{1,0:T(8,128)S(1)}, f32[24,256]{1,0:T(8,128)S(1)}, f32[24,256]{1,0:T(8,128)}, f32[256,256]{1,0:T(8,128)S(1)}) fusion(f32[24,256]{1,0:T(8,128)S(1)} %copy-done.41, f32[256,256]{1,0:T(8,128)S(1)} %copy-done.31, f32[24,256]{1,0:T(8,128)S(1)} %copy-done.43, pred[256,256]{1,0:T(8,128)(4,1)S(1)} %copy-done.33, ...), kind=kOutput, calls=%fused_computation.15 | convolution fusion | flops 1228322816 | bytes 3858432 | tf_op jit(solution)/shard_map/transpose(jvp(vmap(bhts,bshp->bthp)))/dot_general | solution.py:46
  106.0 3.0 fusion.54.refs_1_
  109.3 1.2 copy-done.11
  111.0 1.8 multiply_reduce_fusion.6
  113.1 2.5 multiply_reduce_fusion.5
  115.6 2.0 slice_multiply_fusion.1
  117.6 2.0 slice_multiply_fusion.2
  119.6 2.0 slice_multiply_fusion.3
  121.7 2.5 reduce-window.16
  124.6 1.5 fusion.107
  126.0 4.1 %multiply_reduce_fusion.3 = (f32[1792]{0:T(1024)S(1)}, f32[1792]{0:T(1024)S(1)}, f32[1,256,1792]{1,2,0:T(8,128)S(1)}) fusion(f32[1,256,1792]{1,2,0:T(8,128)} %copy-done.9, f32[1,256,3352]{1,2,0:T(8,128)S(1)} %convolution_bitcast_fusion, f32[1792]{0:T(1024)S(1)} %get-tuple-element.140, f32[1,255,1792]{1,2,0:T(8,128)} %slice_multiply_fusion.1, ...), kind=kLoop, calls=%fused_computation.54 | loop fusion | flops 3207680 | bytes 10988544 | tf_op jit(solution)/shard_map/transpose(jvp(vmap()))/reduce_sum | solution.py:67
  130.4 0.8 copy-done.13
  131.2 5.6 %fusion.33.refs_0_ = f32[768,3328]{1,0:T(8,128)} fusion(bf16[256,3352]{0,1:T(8,128)(2,1)S(1)} %fusion.32, bf16[1,256,768]{2,1,0:T(8,128)(2,1)S(1)} %copy-done.13, f32[768]{0:T(1024)S(1)} %convert_element_type.68, f32[256]{0:T(256)S(1)} %fusion.93), kind=kOutput, calls=%fused_computation.65 | convolution fusion | flops 1309409280 | bytes 12325888 | tf_op jit(solution)/shard_map/td,tk->dk/dot_general | solution.py:372
  137.3 2.6 fusion.47
  140.3 0.7 bitcast_multiply_fusion.2
  142.1 0.9 pad_maximum_fusion.3.refs_2_
  143.0 119.6 %reduce_grads.1 = (f32[192,3328]{1,0:T(8,128)}, f32[384,768]{1,0:T(8,128)}, f32[192,128]{1,0:T(8,128)}) custom-call(f32[768,3328]{1,0:T(8,128)} %fusion.33.refs_0_, f32[1536,768]{1,0:T(8,128)} %fusion.54.refs_1_, f32[768,128]{1,0:T(8,128)} %pad_maximum_fusion.3.refs_2_), custom_call_target="tpu_custom_call" | custom-call | tf_op jit(solution)/shard_map/reduce_grads/pallas_call | solution.py:307
  262.6 1.0 slice.167
  263.6 0.9 slice_bitcast_fusion.10
  264.6 1.2 multiply_reduce_fusion.14
  265.8 0.7 multiply_reduce_fusion.11
  267.1 1.2 multiply_reduce_fusion.12
  268.3 2.2 multiply_reduce_fusion.9
  270.5 4.6 %multiply_reduce_fusion.2 = (f32[]{:T(128)}, f32[192,3352]{1,0:T(8,128)}) fusion(f32[192,24]{1,0:T(8,128)S(1)} %get-tuple-element.183, f32[192,3328]{1,0:T(8,128)} %get-tuple-element.24), kind=kLoop, calls=%fused_computation.45 | loop fusion | flops 1930751 | bytes 5148676 | tf_op jit(solution)/shard_map/reduce_sum | solution.py:104
  279.6 6.4 %psum.7 = f32[]{:T(128)} all-reduce(f32[]{:T(128)S(6)} %add.268), channel_id=1, replica_groups=mesh['grp'=4,'dp'=8] {'grp'}, use_global_device_ids=true, to_apply=%region_29.30 | all-reduce | flops 1 | bytes 8 | tf_op jit(solution)/shard_map/psum | solution.py:417
  286.7 0.7 broadcast_multiply_fusion.3
  288.5 0.7 reshape.759
  289.8 4.1 %fusion.59 = (f32[1,384,768]{2,1,0:T(8,128)}, f32[1,384,768]{2,1,0:T(8,128)}, f32[384,768]{1,0:T(8,128)}) fusion(f32[384,768]{1,0:T(8,128)S(1)} %copy-done.15, f32[]{:T(128)S(6)} %min.3, f32[2,384,768]{2,1,0:T(8,128)} %param.29, f32[384,768]{1,0:T(8,128)S(1)} %copy-done.24), kind=kLoop, calls=%fused_computation.115 | loop fusion | flops 5013504 | bytes 8257540 | tf_op jit(solution)/shard_map/stack | solution.py:98
  293.9 1.5 mul.1065
  295.4 1.4 multiply_subtract_fusion.2
  296.8 0.8 fusion.75
  298.2 1.3 mul.1075
  299.5 1.3 multiply_subtract_fusion.4
  300.9 0.7 multiply_add_fusion.3
  302.2 1.3 multiply_subtract_fusion.3
  303.5 2.3 fusion.49
  305.8 5.6 %multiply_subtract_fusion = f32[192,3352]{1,0:T(8,128)} fusion(f32[192,3352]{1,0:T(8,128)S(1)} %copy-done.14, f32[192,3352]{1,0:T(8,128)} %get-tuple-element.229, f32[2,192,3352]{2,1,0:T(8,128)} %param.25, f32[]{:T(128)S(6)} %min.3), kind=kLoop, calls=%fused_computation.43 | loop fusion | flops 10940928 | bytes 12871684 | tf_op jit(solution)/shard_map/sub | solution.py:97
  312.6 1.4 multiply_add_fusion
  314.1 2.7 pad_maximum_fusion
  317.4 1.6 pad_maximum_fusion.2
  319.5 0.9 copy-done.18
  320.4 1.8 fusion.41
  322.1 1.0 copy.208
  (235 shorter events, 17.9 us)
Async XLA Ops:
  7.2 3.3 copy-start.23
  7.2 47.0 %all-gather.6.cloned.1.call-start = ((), (), s32[]{:S(2)}) async-start(), calls=%async_computation | async-start | bytes 6635520 | tf_op jit(solution)/shard_map/all_gather | solution.py:341
  10.3 10.9 %copy-start.12 = (bf16[1,256,768]{2,1,0:T(8,128)(2,1)S(1)}, bf16[1,256,768]{2,1,0:T(8,128)(2,1)}, u32[]{:S(2)}) copy-start(bf16[1,256,768]{2,1,0:T(8,128)(2,1)} %param.15) | copy-start | bytes 1179652
  10.3 11.7 %copy-start.32 = (f32[5,448]{1,0:T(8,128)S(1)}, f32[5,448]{1,0:T(8,128)}, u32[]{:S(2)}) copy-start(f32[5,448]{1,0:T(8,128)} %param.20) | copy-start | bytes 26884
  10.3 17.3 %copy-start.51 = (f32[3,6]{1,0:T(4,128)S(1)}, f32[3,6]{1,0:T(4,128)}, u32[]{:S(2)}) copy-start(f32[3,6]{1,0:T(4,128)} %param.21) | copy-start | bytes 220
  10.3 23.2 %copy-start.52 = (f32[384]{0:T(512)S(1)}, f32[384]{0:T(512)}, u32[]{:S(2)}) copy-start(f32[384]{0:T(512)} %param.22) | copy-start | bytes 4612
  10.3 28.6 %copy-start.64 = (f32[2,192]{1,0:T(2,128)S(1)}, f32[2,192]{1,0:T(2,128)}, u32[]{:S(2)}) copy-start(f32[2,192]{1,0:T(2,128)} %param.24) | copy-start | bytes 4612
  10.4 29.2 %copy-start.44 = (f32[2,5,448]{2,0,1:T(2,128)S(1)}, f32[2,5,448]{2,0,1:T(2,128)}, u32[]{:S(2)}) copy-start(f32[2,5,448]{2,0,1:T(2,128)} %param.26) | copy-start | bytes 53764
  10.4 29.8 %copy-start.62 = (f32[2,3,6]{2,0,1:T(2,128)S(1)}, f32[2,3,6]{2,0,1:T(2,128)}, u32[]{:S(2)}) copy-start(f32[2,3,6]{2,0,1:T(2,128)} %param.27) | copy-start | bytes 436
  10.4 30.4 %copy-start.34 = (s32[1,256]{1,0:T(1,128)S(1)}, s32[1,256]{1,0:T(1,128)}, u32[]{:S(2)}) copy-start(s32[1,256]{1,0:T(1,128)} %param.16) | copy-start | bytes 3076
  10.4 71.9 %all-gather.8.cloned.1.call-start = ((), (), s32[]{:S(2)}) async-start(), calls=%async_computation.1 | async-start | bytes 2949120 | tf_op jit(solution)/shard_map/all_gather | solution.py:345
  33.4 34.5 %copy-start.54 = (f32[24]{0:T(128)}, f32[24]{0:T(128)S(1)}, u32[]{:S(2)}) copy-start(f32[24]{0:T(128)S(1)} %get-tuple-element.198) | copy-start | bytes 292
  40.9 18.6 %copy-start.45 = (f32[1,256]{1,0:T(1,128)}, f32[1,256]{1,0:T(1,128)S(1)}, u32[]{:S(2)}) copy-start(f32[1,256]{1,0:T(1,128)S(1)} %get-tuple-element.202) | copy-start | bytes 3076
  40.9 18.6 %copy-start.47 = (f32[1,256]{1,0:T(1,128)}, f32[1,256]{1,0:T(1,128)S(1)}, u32[]{:S(2)}) copy-start(f32[1,256]{1,0:T(1,128)S(1)} %get-tuple-element.203) | copy-start | bytes 3076
  59.5 6.0 %copy-start.7 = (f32[1,255,1792]{1,2,0:T(8,128)}, f32[1,255,1792]{1,2,0:T(8,128)S(1)}, u32[]{:S(2)}) copy-start(f32[1,255,1792]{1,2,0:T(8,128)S(1)} %slice.189) | copy-start | bytes 5483524
  65.4 2.5 copy-start.56
  71.7 8.7 %copy-start.3 = (f32[1,256,1792]{1,2,0:T(8,128)S(1)}, f32[1,256,1792]{1,2,0:T(8,128)}, u32[]{:S(2)}) copy-start(f32[1,256,1792]{1,2,0:T(8,128)} %copy-done.2) | copy-start | bytes 5505028
  80.4 1.8 copy-start.21
  82.3 23.7 %copy-start.35 = (f32[256]{0:T(256)}, f32[256]{0:T(256)S(1)}, u32[]{:S(2)}) copy-start(f32[256]{0:T(256)S(1)} %fusion.94) | copy-start | bytes 3076
  82.3 3.4 %copy-start = (f32[1,256,1536]{1,2,0:T(8,128)S(1)}, f32[1,256,1536]{1,2,0:T(8,128)}, u32[]{:S(2)}) copy-start(f32[1,256,1536]{1,2,0:T(8,128)} %get-tuple-element.167) | copy-start | bytes 4718596
  82.3 3.4 %copy-start.4 = (f32[1,256,1792]{1,2,0:T(8,128)S(1)}, f32[1,256,1792]{1,2,0:T(8,128)}, u32[]{:S(2)}) copy-start(f32[1,256,1792]{1,2,0:T(8,128)} %copy-done.2) | copy-start | bytes 5505028
  82.3 3.7 %copy-start.22 = (f32[24,64,256]{2,1,0:T(8,128)S(1)}, f32[24,64,256]{2,1,0:T(8,128)}, u32[]{:S(2)}) copy-start(f32[24,64,256]{2,1,0:T(8,128)} %copy-done.21) | copy-start | bytes 4718596
  86.0 3.2 copy-start.31
  86.0 3.2 copy-start.33
  86.0 3.2 copy-start.41
  86.0 3.2 copy-start.43
  89.2 5.5 %copy-start.29 = (f32[1,256,1536]{1,2,0:T(8,128)S(1)}, f32[1,256,1536]{1,2,0:T(8,128)}, u32[]{:S(2)}) copy-start(f32[1,256,1536]{1,2,0:T(8,128)} %slice.194) | copy-start | bytes 4718596
  94.7 11.2 %copy-start.27 = (bf16[1,256,768]{2,1,0:T(8,128)(2,1)S(1)}, bf16[1,256,768]{2,1,0:T(8,128)(2,1)}, u32[]{:S(2)}) copy-start(bf16[1,256,768]{2,1,0:T(8,128)(2,1)} %param.17) | copy-start | bytes 1179652
  109.0 2.0 copy-start.19
  109.0 2.0 copy-start.48
  111.0 1.8 copy-start.6
  111.0 2.0 copy-start.8
  111.0 2.1 copy-start.46
  112.8 2.8 copy-start.9
  119.6 4.9 %copy-start.55 = (f32[24]{0:T(128)S(1)}, f32[24]{0:T(128)}, u32[]{:S(2)}) copy-start(f32[24]{0:T(128)} %copy-done.54) | copy-start | bytes 292
  119.6 5.0 %copy-start.57 = (f32[24]{0:T(128)S(1)}, f32[24]{0:T(128)}, u32[]{:S(2)}) copy-start(f32[24]{0:T(128)} %get-tuple-element.200) | copy-start | bytes 292
  126.0 4.2 %copy-start.20 = (f32[1,256,1536]{1,2,0:T(8,128)S(1)}, f32[1,256,1536]{1,2,0:T(8,128)}, u32[]{:S(2)}) copy-start(f32[1,256,1536]{1,2,0:T(8,128)} %get-tuple-element.170) | copy-start | bytes 4718596
  130.2 7.0 %slice-start.2 = ((s8[5308416]{0:T(1024)(128)(4,1)}), s8[1114112]{0:T(1024)(128)(4,1)S(1)}, s32[]{:S(2)}) async-start(s8[5308416]{0:T(1024)(128)(4,1)} %bitcast.275), calls=%async_computation.4 | async-start | bytes 2228224
  131.2 6.0 %slice-start.3 = ((s8[5308416]{0:T(1024)(128)(4,1)}), s8[4194304]{0:T(1024)(128)(4,1)S(1)}, s32[]{:S(2)}) async-start(s8[5308416]{0:T(1024)(128)(4,1)} %bitcast.275), calls=%async_computation.5 | async-start | bytes 8388608
  137.2 2.8 copy-start.38
  137.2 2.8 copy-start.37
  137.2 2.8 copy-start.40
  137.2 3.1 copy-start.67
  137.2 3.8 %copy-start.39 = (f32[1536]{0:T(1024)S(1)}, f32[1536]{0:T(1024)}, u32[]{:S(2)}) copy-start(f32[1536]{0:T(1024)} %get-tuple-element.155) | copy-start | bytes 18436
  137.3 4.0 %copy-start.63 = (f32[24]{0:T(128)S(1)}, f32[24]{0:T(128)}, u32[]{:S(2)}) copy-start(f32[24]{0:T(128)} %get-tuple-element.157) | copy-start | bytes 292
  270.5 8.5 %copy-start.61 = (f32[2,384]{1,0:T(2,128)S(1)}, f32[2,384]{1,0:T(2,128)}, u32[]{:S(2)}) copy-start(f32[2,384]{1,0:T(2,128)} %param.28) | copy-start | bytes 9220
  270.5 17.4 %copy-start.50 = (f32[256]{0:T(256)S(1)}, f32[256]{0:T(256)}, u32[]{:S(2)}) copy-start(f32[256]{0:T(256)} %copy-done.49) | copy-start | bytes 3076
  270.5 19.3 %copy-start.15 = (f32[384,768]{1,0:T(8,128)S(1)}, f32[384,768]{1,0:T(8,128)}, u32[]{:S(2)}) copy-start(f32[384,768]{1,0:T(8,128)} %get-tuple-element.233) | copy-start | bytes 3538948
  270.5 19.3 %copy-start.24 = (f32[384,768]{1,0:T(8,128)S(1)}, f32[384,768]{1,0:T(8,128)}, u32[]{:S(2)}) copy-start(f32[384,768]{1,0:T(8,128)} %param.23) | copy-start | bytes 3538948
  289.8 13.7 %copy-start.28 = (bf16[1,256,768]{2,1,0:T(8,128)(2,1)S(1)}, bf16[1,256,768]{2,1,0:T(8,128)(2,1)}, u32[]{:S(2)}) copy-start(bf16[1,256,768]{2,1,0:T(8,128)(2,1)} %param.17) | copy-start | bytes 1179652
  293.9 11.9 %copy-start.14 = (f32[192,3352]{1,0:T(8,128)S(1)}, f32[192,3352]{1,0:T(8,128)}, u32[]{:S(2)}) copy-start(f32[192,3352]{1,0:T(8,128)} %param.19) | copy-start | bytes 7723012
  305.8 6.8 %slice-start = ((s8[5308416]{0:T(1024)(128)(4,1)}), s8[4194304]{0:T(1024)(128)(4,1)S(1)}, s32[]{:S(2)}) async-start(s8[5308416]{0:T(1024)(128)(4,1)} %bitcast.270), calls=%async_computation.2 | async-start | bytes 8388608
  305.8 5.6 %copy-start.58 = (f32[192]{0:T(256)S(1)}, f32[192]{0:T(256)}, u32[]{:S(2)}) copy-start(f32[192]{0:T(256)} %get-tuple-element.228) | copy-start | bytes 2308
  305.8 5.6 %copy-start.59 = (f32[1,192]{1,0:T(1,128)S(1)}, f32[1,192]{1,0:T(1,128)}, u32[]{:S(2)}) copy-start(f32[1,192]{1,0:T(1,128)} %get-tuple-element.196) | copy-start | bytes 2308
  305.8 5.6 %copy-start.60 = (f32[1,192]{1,0:T(1,128)S(1)}, f32[1,192]{1,0:T(1,128)}, u32[]{:S(2)}) copy-start(f32[1,192]{1,0:T(1,128)} %get-tuple-element.197) | copy-start | bytes 2308
  305.8 5.6 %copy-start.66 = (f32[192]{0:T(256)S(1)}, f32[192]{0:T(256)}, u32[]{:S(2)}) copy-start(f32[192]{0:T(256)} %param.18) | copy-start | bytes 2308
  305.8 6.8 %slice-start.1 = ((s8[5308416]{0:T(1024)(128)(4,1)}), s8[1114112]{0:T(1024)(128)(4,1)S(1)}, s32[]{:S(2)}) async-start(s8[5308416]{0:T(1024)(128)(4,1)} %bitcast.270), calls=%async_computation.3 | async-start | bytes 2228224
  305.8 6.8 %copy-start.17 = (f32[192,3328]{1,0:T(8,128)S(1)}, f32[192,3328]{1,0:T(8,128)}, u32[]{:S(2)}) copy-start(f32[192,3328]{1,0:T(8,128)} %get-tuple-element.24) | copy-start | bytes 7667716
  314.0 3.3 %copy-start.25 = (f32[1,384,768]{2,1,0:T(8,128)S(1)}, f32[1,384,768]{2,1,0:T(8,128)}, u32[]{:S(2)}) copy-start(f32[1,384,768]{2,1,0:T(8,128)} %get-tuple-element.173) | copy-start | bytes 3538948
  314.0 3.3 %copy-start.26 = (f32[1,384,768]{2,1,0:T(8,128)S(1)}, f32[1,384,768]{2,1,0:T(8,128)}, u32[]{:S(2)}) copy-start(f32[1,384,768]{2,1,0:T(8,128)} %get-tuple-element.174) | copy-start | bytes 3538948
  317.4 2.1 copy-start.1
  317.4 3.0 copy-start.18
  317.4 3.0 copy-start.36
  320.4 1.8 copy-start.16
  (11 other events, 12.2 us)
Sparse Core Ops, SparseCore 0:
  10.4 43.7 all-gather.5
  56.3 24.0 all-gather.7

commit v2 on v1

--- a/solution.py
+++ b/solution.py
@@ -24,7 +24,7 @@
 
 
 def scan_blocks(head_vals, step_size, log_rate, write_proj, read_proj, seg_row):
-    highest = lax.Precision.HIGHEST
+    highest = lax.Precision.HIGH
     length, head_count, head_width = head_vals.shape
     blocks = length // STRETCH
     block_vals = head_vals.reshape(blocks, STRETCH, head_count, head_width)
@@ -98,6 +98,54 @@
     return (updated, jnp.stack([first, second_root]))
 
 
+def update_body(count, widths, clip_ref, *refs):
+    grads = refs[:count]
+    master_ref, moment_ref, grad_out, master_out, moment_out = refs[count:]
+    clip_factor = clip_ref[0, 0]
+    start = 0
+    for grad_ref, width in zip(grads, widths):
+        cols = slice(start, start + width)
+        grad = grad_ref[:, :width]
+        master = master_ref[:, cols]
+        grad_out[:, cols] = grad
+        clipped = grad * clip_factor
+        first = beta_first * moment_ref[0, :, cols] + (1.0 - beta_first) * clipped
+        root = moment_ref[1, :, cols]
+        second_root = jnp.sqrt(beta_second * root * root + (1.0 - beta_second) * clipped * clipped)
+        first_hat = first / (1.0 - beta_first**STEP)
+        root_hat = second_root / ((1.0 - beta_second**STEP) ** 0.5)
+        step = first_hat / (root_hat + adam_eps) + weight_decay * master
+        master_out[:, cols] = master - learn_rate * step
+        moment_out[0, :, cols] = first
+        moment_out[1, :, cols] = second_root
+        start += width
+
+
+def update_weight(master, moments, grads, widths, clip_factor, name):
+    rows, cols = master.shape
+    height = 24 if rows % 24 == 0 else rows
+    if cols < 1024 and rows % 96 == 0:
+        height = 96
+    wide = jnp.float32
+    row_spec = pl.BlockSpec((height, cols), lambda i: (i, 0))
+    pair_spec = pl.BlockSpec((2, height, cols), lambda i: (0, i, 0))
+    return pl.pallas_call(
+        lambda *refs: update_body(len(grads), widths, *refs),
+        grid=(rows // height,),
+        out_shape=[
+            jax.ShapeDtypeStruct((rows, cols), wide),
+            jax.ShapeDtypeStruct((rows, cols), wide),
+            jax.ShapeDtypeStruct((2, rows, cols), wide),
+        ],
+        in_specs=[pl.BlockSpec(memory_space=pltpu.SMEM)]
+        + [pl.BlockSpec((height, grad.shape[1]), lambda i: (i, 0)) for grad in grads]
+        + [row_spec, pair_spec],
+        out_specs=[row_spec, row_spec, pair_spec],
+        compiler_params=pltpu.CompilerParams(vmem_limit_bytes=40 * 1024 * 1024),
+        name=name,
+    )(clip_factor.reshape(1, 1), *grads, master, moments)
+
+
 def square_sum(arrays):
     total = jnp.zeros((), jnp.float32)
     for grad_arr in arrays:
@@ -405,7 +453,6 @@
         reduced = [piece + lax.ppermute(piece, "dp", pairs) for piece in reduced]
         step *= 2
     main_sum, out_grad_w, last_sum = reduced
-    in_grad = jnp.concatenate([main_sum, last_sum[:, :tail_cols]], axis=1)
     flat = last_sum[:, tail_cols:].reshape(-1)
     norm_grad = flat[:own_rows]
     gate_grad = flat[own_rows : own_rows + gate_size]
@@ -413,15 +460,24 @@
     head_at = conv_at + grad_conv.shape[0] * conv_cols
     conv_grad = flat[conv_at:head_at].reshape(-1, conv_cols)
     head_grad = flat[head_at:small_size].reshape(-1, head_cols)
-    local_squares = square_sum((norm_grad, in_grad, conv_grad, head_grad, gate_grad, out_grad_w))
+    local_squares = square_sum((main_sum, out_grad_w, last_sum))
     squares = lax.psum(local_squares, "grp")
     clip_factor = jnp.minimum(1.0, clip_limit / jnp.sqrt(squares + 1e-06))
     norm_new, norm_mom = adam_update(norm_gain, norm_gain_moments, norm_grad, clip_factor)
-    in_new, in_mom = adam_update(in_weight, in_weight_moments, in_grad, clip_factor)
+    in_grad, in_new, in_mom = update_weight(
+        in_weight,
+        in_weight_moments,
+        (main_sum, last_sum),
+        (main_cols, tail_cols),
+        clip_factor,
+        "update_in",
+    )
     conv_new, conv_mom = adam_update(conv_params, conv_params_moments, conv_grad, clip_factor)
     head_new, head_mom = adam_update(head_params, head_params_moments, head_grad, clip_factor)
     gate_new, gate_mom = adam_update(gate_gain, gate_gain_moments, gate_grad, clip_factor)
-    out_new, out_mom = adam_update(out_weight, out_weight_moments, out_grad_w, clip_factor)
+    out_grad_w, out_new, out_mom = update_weight(
+        out_weight, out_weight_moments, (out_grad_w,), (width,), clip_factor, "update_out"
+    )
     return (
         block_out,
         input_grad,

time: 336 us -> 304 us (0.905); the launches traced: 330 us -> 303 us
  other arithmetic: 74.6 us -> 48.1 us
  Pallas kernels: 120 us -> 130 us
  matrix products: 48.3 us -> 42 us
    pallas_call x0 -> x2, Pallas kernels: none -> 8.77 us  [update_weight(): pl.pallas_call(lambda *refs: update_body(len(grads), widths, *refs), grid...]
    another operation x7 -> x4, other arithmetic: 9.54 us -> 1.18 us  [adam_update(): return (updated, jnp.stack([first, second_root]))]
    dot_general x3, matrix products: 24.7 us -> 16.3 us  [scan_blocks(): jnp.einsum('bhts,bshp->bthp', weighted, block_vals, precision=highest)]
    sub x5 -> x4, other arithmetic: 10.2 us -> 2.5 us  [adam_update(): master - learn_rate * (first_hat / (root_hat + adam_eps) + weight_decay *...]
    reduce_sum x6 -> x3, other arithmetic: 10.4 us -> 5.55 us  [square_sum(): total = total + jnp.sum(grad_arr * grad_arr)]
    unnamed x153 -> x172, local copies, waits for them, and re-layouts: 12 us -> 13.5 us
where the time goes in v2:
time: 304 us; the launch traced here: 303 us
  Pallas kernels  130 us (43%)
  other arithmetic  48.1 us (16%)
  matrix products  42 us (14%)
  blocking collectives  30.6 us (10%)
  local copies, waits for them, and re-layouts  21.9 us (7%)
  between operations  18.4 us (6%)
  waiting for transfers between devices  12.5 us (4%)
    pallas_call x1, Pallas kernels, reduce_grads(): pl.pallas_call(lambda *refs: reduce_body(shapes, plan, *refs), out_shape=...  121 us
    dot_general x3, matrix products, scan_blocks(): jnp.einsum('bhts,bshp->bthp', weighted, block_vals, precision=highest)  16.3 us
    unnamed x172, local copies, waits for them, and re-layouts  13.5 us
    all_gather x1, waiting for transfers between devices, shards(): lax.all_gather(in_weight.astype(half), 'grp', axis=0, tiled=True)  12.4 us
    pallas_call x2, Pallas kernels, update_weight(): pl.pallas_call(lambda *refs: update_body(len(grads), widths, *refs), grid...  8.77 us
    unnamed x1, blocking collectives  8.34 us
    psum x1, blocking collectives, shards(): squares = lax.psum(local_squares, 'grp')  6.17 us
    mul x4, other arithmetic, mix_one(): summed = summed + conv_arr[kernel - 1 - offset] * shifted * keep_mask  6.15 us
  transfers between devices with their start and end apart: 2, of which 1 were waited for; matrix products, arithmetic and copies ran while one was open for 9% of the time, Pallas kernels for 0%

profile of v2, /device:TPU:0, one launch (start us, length us, event | category | flops | bytes accessed | tf_op | source)
XLA Modules:
  0.0 303.5 jit_solution(16483621662211404024)
XLA Ops:
  7.2 3.0 %convert_element_type.70 = bf16[192,3352]{1,0:T(8,128)(2,1)} convert(f32[192,3352]{1,0:T(8,128)} %refs_3_.2) | non-fusion elementwise | flops 643584 | bytes 3861504 | tf_op jit(solution)/shard_map/convert_element_type | solution.py:389
  10.5 0.9 convert_element_type.77
  11.4 0.6 dynamic-slice
  12.9 8.3 %all-reduce.23 = bf16[768]{0:T(1024)(128)(2,1)S(1)} all-reduce(bf16[768]{0:T(1024)(128)(2,1)S(1)} %dynamic-update-slice), channel_id=1, replica_groups=mesh['grp'=4,'dp'=8] {'grp'}, use_global_device_ids=true, to_apply=%add.23 | all-reduce | flops 768 | bytes 3072
  22.0 5.5 %all-gather = bf16[4,448,5]{1,2,0:T(8,128)(2,1)S(1)} all-gather(bf16[1,448,5]{1,2,0:T(8,128)(2,1)S(1)} %convert_bitcast_fusion), channel_id=1, replica_groups=mesh['grp'=4,'dp'=8] {'grp'}, dimensions={0}, use_global_device_ids=true | all-gather | bytes 22400 | tf_op jit(solution)/shard_map/all_gather | solution.py:390
  27.7 5.2 %all-gather.1 = bf16[4,6,3]{1,2,0:T(4,128)(2,1)S(1)} all-gather(bf16[1,6,3]{1,2,0:T(4,128)(2,1)S(1)} %convert_bitcast_fusion.1), channel_id=1, replica_groups=mesh['grp'=4,'dp'=8] {'grp'}, dimensions={0}, use_global_device_ids=true | all-gather | bytes 180 | tf_op jit(solution)/shard_map/all_gather | solution.py:391
  33.8 5.3 %all-gather.2 = bf16[4,1,384]{2,1,0:T(2,128)(2,1)S(1)} all-gather(bf16[1,1,384]{2,1,0:T(2,128)(2,1)S(1)} %reshape.727), channel_id=1, replica_groups=mesh['grp'=4,'dp'=8] {'grp'}, dimensions={0}, use_global_device_ids=true | all-gather | bytes 3840 | tf_op jit(solution)/shard_map/all_gather | solution.py:392
  39.2 0.6 fusion.100
  40.5 0.6 multiply_reduce_fusion.12
  41.1 0.7 fusion.47
  41.8 12.4 %all-gather.6.cloned.1.call-done = bf16[768,3352]{1,0:T(8,128)(2,1)} async-done(((bf16[192,3352]{1,0:T(8,128)(2,1)}), bf16[768,3352]{1,0:T(8,128)(2,1)}) %all-gather.6.cloned.1.call-update) | async-done | bytes 5148688 | tf_op jit(solution)/shard_map/all_gather | solution.py:389
  54.2 4.8 %convolution_bitcast_fusion = f32[1,256,3352]{1,2,0:T(8,128)S(1)} fusion(bf16[768,3352]{1,0:T(8,128)(2,1)} %all-gather.6.cloned.1.call-done, bf16[1,256,768]{2,1,0:T(8,128)(2,1)} %param.15, f32[768]{0:T(1024)S(1)} %convert_element_type.68, f32[256]{0:T(256)S(1)} %fusion.80), kind=kOutput, calls=%fused_computation.8 | convolution fusion | flops 1318846464 | bytes 8978432 | tf_op jit(solution)/shard_map/dot_general | solution.py:403
  59.5 0.9 copy-done.19
  60.4 0.6 copy-done.14
  61.1 3.8 %fusion.22 = (f32[1,256,1792]{1,2,0:T(8,128)S(1)}, f32[1,256,1792]{1,2,0:T(8,128)}) fusion(f32[256]{0:T(256)S(1)} %bitcast.260, f32[1,253,1792]{1,2,0:T(8,128)S(1)} %slice.171, f32[1792]{0:T(1024)S(1)} %get-tuple-element.149, f32[256]{0:T(256)S(1)} %bitcast.258, f32[1,254,1792]{1,2,0:T(8,128)S(1)} %slice.169, f32[1792]{0:T(1024)S(1)} %get-tuple-element.150, ...), kind=kLoop, calls=%fused_computation.39 | loop fusion | flops 6881280 | bytes 11005952 | tf_op jit(solution)/shard_map/jvp(vmap(jit(silu)))/mul | solution.py:77
  64.9 1.2 copy-done.11
  66.1 1.2 slice.172
  67.4 0.7 multiply_bitcast_fusion
  68.7 0.7 slice_reduce_fusion.1
  69.4 0.7 reduce-window.15
  70.1 0.7 copy.110
  70.8 0.8 broadcast.366
  71.6 1.3 fusion.49
  72.9 0.7 copy-done.31
  73.6 5.6 %fusion.4 = f32[24,64,256]{2,1,0:T(8,128)S(1)} fusion(f32[256,24,64]{0,2,1:T(8,128)} %bitcast.244, f32[24,256]{1,0:T(8,128)} %get-tuple-element.181, f32[256,256]{1,0:T(8,128)S(1)} %fusion.49, f32[24,256]{1,0:T(8,128)S(1)} %bitcast_add_fusion.2, pred[256,256]{1,0:T(8,128)(4,1)} %fusion.47), kind=kOutput, calls=%fused_computation.7 | convolution fusion | flops 610271232 | bytes 3522560 | tf_op jit(solution)/shard_map/jvp(vmap(bhts,bshp->bthp))/dot_general | solution.py:46
  79.2 1.8 multiply_reduce_fusion.8
  81.1 4.0 %fusion.28 = (f32[1536]{0:T(1024)}, f32[256]{0:T(256)S(1)}, f32[256,1536]{0,1:T(8,128)S(1)}) fusion(f32[1,256,1536]{1,2,0:T(8,128)} %get-tuple-element.175, f32[256]{0:T(256)S(1)} %fusion.81, f32[1536]{0:T(1024)S(1)} %reshape.729, bf16[1536,768]{1,0:T(8,128)(2,1)} %all-gather.8.cloned.1.call-done, bf16[1,256,768]{2,1,0:T(8,128)(2,1)} %param.17), kind=kOutput, calls=%fused_computation.49 | convolution fusion | flops 606337280 | bytes 5912576 | tf_op jit(solution)/shard_map/td,id->ti/dot_general | solution.py:416
  85.1 3.1 %multiply_reduce_fusion.7 = (f32[1536]{0:T(1024)}, f32[1,256,1536]{1,2,0:T(8,128)S(1)}, f32[1,256,1536]{1,2,0:T(8,128)}) fusion(f32[1,256,1792]{1,2,0:T(8,128)S(1)} %copy-done.13, f32[1,256,3352]{1,2,0:T(8,128)S(1)} %convolution_bitcast_fusion, f32[1,256,1536]{1,2,0:T(8,128)S(1)} %copy-done.9, f32[256]{0:T(256)S(1)} %multiply_multiply_fusion.13, ...), kind=kLoop, calls=%fused_computation.57 | loop fusion | flops 8256000 | bytes 11030528 | tf_op jit(solution)/shard_map/transpose(jvp(vmap()))/reduce_sum | solution.py:84
  88.3 3.2 %fusion.2 = f32[24,64,256]{2,1,0:T(8,128)S(1)} fusion(f32[24,64,256]{2,1,0:T(8,128)S(1)} %bitcast.240, f32[24,256]{1,0:T(8,128)S(1)} %copy-done.47, f32[256,256]{1,0:T(8,128)S(1)} %copy-done.32, f32[24,256]{1,0:T(8,128)S(1)} %copy-done.49, pred[256,256]{1,0:T(8,128)(4,1)S(1)} %copy-done.38), kind=kOutput, calls=%fused_computation.6 | convolution fusion | flops 610271232 | bytes 3522560 | tf_op jit(solution)/shard_map/transpose(jvp(vmap(bhts,bshp->bthp)))/dot_general | solution.py:46
  91.4 7.6 %fusion.7 = (f32[24,256]{1,0:T(8,128)S(1)}, f32[24,256]{1,0:T(8,128)S(1)}, f32[24,256]{1,0:T(8,128)}, f32[256,256]{1,0:T(8,128)S(1)}) fusion(f32[24,256]{1,0:T(8,128)S(1)} %copy-done.47, f32[256,256]{1,0:T(8,128)S(1)} %copy-done.32, f32[24,256]{1,0:T(8,128)S(1)} %copy-done.49, pred[256,256]{1,0:T(8,128)(4,1)S(1)} %copy-done.38, ...), kind=kOutput, calls=%fused_computation.10 | convolution fusion | flops 624343040 | bytes 3858432 | tf_op jit(solution)/shard_map/transpose(jvp(vmap(bhts,bshp->bthp)))/dot_general | solution.py:46
  99.6 3.0 fusion.43.refs_1_
  102.9 1.2 copy-done.20
  104.7 1.8 multiply_reduce_fusion.6
  106.7 2.5 multiply_reduce_fusion.5
  109.2 2.0 slice_multiply_fusion
  111.2 2.0 slice_multiply_fusion.1
  113.2 2.0 slice_multiply_fusion.2
  115.3 2.5 reduce-window.16
  118.2 1.5 fusion.94
  119.7 4.2 %multiply_reduce_fusion.3 = (f32[1792]{0:T(1024)S(1)}, f32[1792]{0:T(1024)S(1)}, f32[1,256,1792]{1,2,0:T(8,128)S(1)}) fusion(f32[1,256,1792]{1,2,0:T(8,128)} %copy-done.18, f32[1,256,3352]{1,2,0:T(8,128)S(1)} %convolution_bitcast_fusion, f32[1792]{0:T(1024)S(1)} %get-tuple-element.152, f32[1,255,1792]{1,2,0:T(8,128)} %slice_multiply_fusion, ...), kind=kLoop, calls=%fused_computation.33 | loop fusion | flops 3207680 | bytes 10988544 | tf_op jit(solution)/shard_map/transpose(jvp(vmap()))/reduce_sum | solution.py:67
  124.1 0.8 copy-done.22
  124.9 5.6 %fusion.24.refs_0_ = f32[768,3328]{1,0:T(8,128)} fusion(bf16[256,3352]{0,1:T(8,128)(2,1)S(1)} %fusion.23, bf16[1,256,768]{2,1,0:T(8,128)(2,1)S(1)} %copy-done.22, f32[768]{0:T(1024)S(1)} %convert_element_type.68, f32[256]{0:T(256)S(1)} %fusion.80), kind=kOutput, calls=%fused_computation.42 | convolution fusion | flops 1309409280 | bytes 12325888 | tf_op jit(solution)/shard_map/td,tk->dk/dot_general | solution.py:420
  131.0 2.6 fusion.36
  134.0 0.7 bitcast_multiply_fusion.2
  135.8 0.9 pad_maximum_fusion.refs_2_
  136.7 121.2 %reduce_grads.1 = (f32[192,3328]{1,0:T(8,128)}, f32[384,768]{1,0:T(8,128)}, f32[192,128]{1,0:T(8,128)}) custom-call(f32[768,3328]{1,0:T(8,128)} %fusion.24.refs_0_, f32[1536,768]{1,0:T(8,128)} %fusion.43.refs_1_, f32[768,128]{1,0:T(8,128)} %pad_maximum_fusion.refs_2_), custom_call_target="tpu_custom_call" | custom-call | tf_op jit(solution)/shard_map/reduce_grads/pallas_call | solution.py:355
  258.0 3.1 %multiply_reduce_fusion.2 = f32[]{:T(128)} fusion(f32[192,3328]{1,0:T(8,128)} %get-tuple-element.30.refs_1_), kind=kLoop, calls=%fused_computation.25 | loop fusion | flops 1277951 | bytes 2555908 | tf_op jit(solution)/shard_map/reduce_sum | solution.py:152
  261.2 0.9 multiply_reduce_fusion.9
  262.1 1.5 multiply_reduce_fusion.10
  265.5 1.0 slice.150
  266.5 6.2 %psum.7 = f32[]{:T(128)} all-reduce(f32[]{:T(128)S(6)} %add.220), channel_id=1, replica_groups=mesh['grp'=4,'dp'=8] {'grp'}, use_global_device_ids=true, to_apply=%region_26.27 | all-reduce | flops 1 | bytes 8 | tf_op jit(solution)/shard_map/psum | solution.py:464
  273.8 1.7 copy-done.1
  275.5 2.5 copy-done.2
  278.0 5.9 %update_in.1 = (f32[192,3352]{1,0:T(8,128)}, f32[192,3352]{1,0:T(8,128)}, f32[2,192,3352]{2,1,0:T(8,128)}) custom-call(f32[1,1]{1,0:T(1,128)} %bitcast.59.refs_0_, f32[192,3328]{1,0:T(8,128)S(1)} %copy-done.1, f32[192,128]{1,0:T(8,128)S(1)} %copy-done.8, f32[192,3352]{1,0:T(8,128)S(1)} %copy-done, f32[2,192,3352]{2,1,0:T(8,128)S(1)} %copy-done.2), custom_call_target="tpu_custom_call" | custom-call | tf_op jit(solution)/shard_map/update_in/pallas_call | solution.py:132
  284.0 2.9 update_out.1
  287.0 0.6 multiply_subtract_fusion
  287.7 0.6 copy.123
  288.4 0.6 multiply_subtract_fusion.2
  289.6 0.7 multiply_subtract_fusion.1
  290.3 1.1 fusion.38
  291.5 0.6 multiply_subtract_fusion.3
  292.0 0.6 pad_maximum_fusion.4
  292.6 0.6 pad_maximum_fusion.3
  293.2 3.4 %fusion.32 = bf16[1,256,768]{2,1,0:T(8,128)(2,1)} fusion(bf16[1536,768]{1,0:T(8,128)(2,1)} %all-gather.8.cloned.1.call-done, bf16[1,256,768]{2,1,0:T(8,128)(2,1)S(1)} %copy-done.22, f32[1,256,1536]{1,2,0:T(8,128)S(1)} %copy-done.10, f32[1536]{0:T(1024)S(1)} %reshape.729, f32[256]{0:T(256)S(1)} %copy-done.41), kind=kOutput, calls=%fused_computation.63 | convolution fusion | flops 605749248 | bytes 4725760 | tf_op jit(solution)/shard_map/dot_general | solution.py:412
  (246 shorter events, 9.3 us)
Async XLA Ops:
  7.2 3.3 %copy-start.3 = (f32[384,768]{1,0:T(8,128)S(1)}, f32[384,768]{1,0:T(8,128)}, u32[]{:S(2)}) copy-start(f32[384,768]{1,0:T(8,128)} %refs_2_.1) | copy-start | bytes 3538948
  7.2 47.0 %all-gather.6.cloned.1.call-start = ((), (), s32[]{:S(2)}) async-start(), calls=%async_computation | async-start | bytes 6635520 | tf_op jit(solution)/shard_map/all_gather | solution.py:389
  10.3 11.0 %copy-start.21 = (bf16[1,256,768]{2,1,0:T(8,128)(2,1)S(1)}, bf16[1,256,768]{2,1,0:T(8,128)(2,1)}, u32[]{:S(2)}) copy-start(bf16[1,256,768]{2,1,0:T(8,128)(2,1)} %param.15) | copy-start | bytes 1179652
  10.3 11.7 %copy-start.36 = (f32[5,448]{1,0:T(8,128)S(1)}, f32[5,448]{1,0:T(8,128)}, u32[]{:S(2)}) copy-start(f32[5,448]{1,0:T(8,128)} %param.20) | copy-start | bytes 26884
  10.3 17.4 %copy-start.64 = (f32[3,6]{1,0:T(4,128)S(1)}, f32[3,6]{1,0:T(4,128)}, u32[]{:S(2)}) copy-start(f32[3,6]{1,0:T(4,128)} %param.21) | copy-start | bytes 220
  10.3 23.4 %copy-start.66 = (f32[384]{0:T(512)S(1)}, f32[384]{0:T(512)}, u32[]{:S(2)}) copy-start(f32[384]{0:T(512)} %param.22) | copy-start | bytes 4612
  10.3 28.8 %copy-start.76 = (f32[2,192]{1,0:T(2,128)S(1)}, f32[2,192]{1,0:T(2,128)}, u32[]{:S(2)}) copy-start(f32[2,192]{1,0:T(2,128)} %param.24) | copy-start | bytes 4612
  10.4 29.4 %copy-start.50 = (f32[2,5,448]{2,0,1:T(2,128)S(1)}, f32[2,5,448]{2,0,1:T(2,128)}, u32[]{:S(2)}) copy-start(f32[2,5,448]{2,0,1:T(2,128)} %param.26) | copy-start | bytes 53764
  10.4 29.4 %copy-start.74 = (f32[2,3,6]{2,0,1:T(2,128)S(1)}, f32[2,3,6]{2,0,1:T(2,128)}, u32[]{:S(2)}) copy-start(f32[2,3,6]{2,0,1:T(2,128)} %param.27) | copy-start | bytes 436
  10.4 30.0 %copy-start.39 = (s32[1,256]{1,0:T(1,128)S(1)}, s32[1,256]{1,0:T(1,128)}, u32[]{:S(2)}) copy-start(s32[1,256]{1,0:T(1,128)} %param.16) | copy-start | bytes 3076
  10.4 30.1 %copy-start.73 = (f32[2,384]{1,0:T(2,128)S(1)}, f32[2,384]{1,0:T(2,128)}, u32[]{:S(2)}) copy-start(f32[2,384]{1,0:T(2,128)} %param.28) | copy-start | bytes 9220
  10.4 70.7 %all-gather.8.cloned.1.call-start = ((), (), s32[]{:S(2)}) async-start(), calls=%async_computation.1 | async-start | bytes 2949120 | tf_op jit(solution)/shard_map/all_gather | solution.py:393
  27.7 31.8 %copy-start.33 = (f32[1792]{0:T(1024)}, f32[1792]{0:T(1024)S(1)}, u32[]{:S(2)}) copy-start(f32[1792]{0:T(1024)S(1)} %get-tuple-element.151) | copy-start | bytes 21508
  33.6 33.8 %copy-start.69 = (f32[24]{0:T(128)}, f32[24]{0:T(128)S(1)}, u32[]{:S(2)}) copy-start(f32[24]{0:T(128)S(1)} %get-tuple-element.199) | copy-start | bytes 292
  40.4 19.0 %copy-start.53 = (f32[1,256]{1,0:T(1,128)}, f32[1,256]{1,0:T(1,128)S(1)}, u32[]{:S(2)}) copy-start(f32[1,256]{1,0:T(1,128)S(1)} %get-tuple-element.202) | copy-start | bytes 3076
  40.5 19.0 %copy-start.55 = (f32[1,256]{1,0:T(1,128)}, f32[1,256]{1,0:T(1,128)S(1)}, u32[]{:S(2)}) copy-start(f32[1,256]{1,0:T(1,128)S(1)} %get-tuple-element.203) | copy-start | bytes 3076
  40.5 19.0 %copy-start.57 = (f32[1,256]{1,0:T(1,128)}, f32[1,256]{1,0:T(1,128)S(1)}, u32[]{:S(2)}) copy-start(f32[1,256]{1,0:T(1,128)S(1)} %get-tuple-element.204) | copy-start | bytes 3076
  59.5 5.4 %copy-start.16 = (f32[1,255,1792]{1,2,0:T(8,128)}, f32[1,255,1792]{1,2,0:T(8,128)S(1)}, u32[]{:S(2)}) copy-start(f32[1,255,1792]{1,2,0:T(8,128)S(1)} %slice.167) | copy-start | bytes 5483524
  73.6 5.6 %copy-start.12 = (f32[1,256,1792]{1,2,0:T(8,128)S(1)}, f32[1,256,1792]{1,2,0:T(8,128)}, u32[]{:S(2)}) copy-start(f32[1,256,1792]{1,2,0:T(8,128)} %copy-done.11) | copy-start | bytes 5505028
  81.0 18.5 %copy-start.40 = (f32[256]{0:T(256)}, f32[256]{0:T(256)S(1)}, u32[]{:S(2)}) copy-start(f32[256]{0:T(256)S(1)} %fusion.81) | copy-start | bytes 3076
  81.1 4.0 %copy-start.9 = (f32[1,256,1536]{1,2,0:T(8,128)S(1)}, f32[1,256,1536]{1,2,0:T(8,128)}, u32[]{:S(2)}) copy-start(f32[1,256,1536]{1,2,0:T(8,128)} %get-tuple-element.175) | copy-start | bytes 4718596
  81.1 4.0 %copy-start.13 = (f32[1,256,1792]{1,2,0:T(8,128)S(1)}, f32[1,256,1792]{1,2,0:T(8,128)}, u32[]{:S(2)}) copy-start(f32[1,256,1792]{1,2,0:T(8,128)} %copy-done.11) | copy-start | bytes 5505028
  81.1 4.0 %copy-start.26 = (f32[24,64,256]{2,1,0:T(8,128)S(1)}, f32[24,64,256]{2,1,0:T(8,128)}, u32[]{:S(2)}) copy-start(f32[24,64,256]{2,1,0:T(8,128)} %copy-done.25) | copy-start | bytes 4718596
  85.1 3.1 %copy-start.32 = (f32[256,256]{1,0:T(8,128)S(1)}, f32[256,256]{1,0:T(8,128)}, u32[]{:S(2)}) copy-start(f32[256,256]{1,0:T(8,128)} %copy-done.31) | copy-start | bytes 786436
  85.1 3.1 %copy-start.38 = (pred[256,256]{1,0:T(8,128)(4,1)S(1)}, pred[256,256]{1,0:T(8,128)(4,1)}, u32[]{:S(2)}) copy-start(pred[256,256]{1,0:T(8,128)(4,1)} %fusion.47) | copy-start | bytes 196612
  85.1 3.1 %copy-start.47 = (f32[24,256]{1,0:T(8,128)S(1)}, f32[24,256]{1,0:T(8,128)}, u32[]{:S(2)}) copy-start(f32[24,256]{1,0:T(8,128)} %get-tuple-element.181) | copy-start | bytes 73732
  85.1 3.1 %copy-start.49 = (f32[24,256]{1,0:T(8,128)S(1)}, f32[24,256]{1,0:T(8,128)}, u32[]{:S(2)}) copy-start(f32[24,256]{1,0:T(8,128)} %copy-done.48) | copy-start | bytes 73732
  88.2 3.2 %copy-start.29 = (f32[1,256,1536]{1,2,0:T(8,128)S(1)}, f32[1,256,1536]{1,2,0:T(8,128)}, u32[]{:S(2)}) copy-start(f32[1,256,1536]{1,2,0:T(8,128)} %slice.172) | copy-start | bytes 4718596
  91.4 8.2 %copy-start.27 = (bf16[1,256,768]{2,1,0:T(8,128)(2,1)S(1)}, bf16[1,256,768]{2,1,0:T(8,128)(2,1)}, u32[]{:S(2)}) copy-start(bf16[1,256,768]{2,1,0:T(8,128)(2,1)} %param.17) | copy-start | bytes 1179652
  106.4 2.8 copy-start.18
  119.7 4.2 %copy-start.24 = (f32[1,256,1536]{1,2,0:T(8,128)S(1)}, f32[1,256,1536]{1,2,0:T(8,128)}, u32[]{:S(2)}) copy-start(f32[1,256,1536]{1,2,0:T(8,128)} %get-tuple-element.178) | copy-start | bytes 4718596
  123.9 7.0 %slice-start = ((s8[5308416]{0:T(1024)(128)(4,1)}), s8[1114112]{0:T(1024)(128)(4,1)S(1)}, s32[]{:S(2)}) async-start(s8[5308416]{0:T(1024)(128)(4,1)} %bitcast.242), calls=%async_computation.2 | async-start | bytes 2228224
  124.9 6.0 %slice-start.1 = ((s8[5308416]{0:T(1024)(128)(4,1)}), s8[4194304]{0:T(1024)(128)(4,1)S(1)}, s32[]{:S(2)}) async-start(s8[5308416]{0:T(1024)(128)(4,1)} %bitcast.242), calls=%async_computation.3 | async-start | bytes 8388608
  130.9 2.8 copy-start.42
  130.9 2.8 copy-start.44
  130.9 2.8 copy-start.43
  130.9 2.8 copy-start.46
  130.9 3.1 %copy-start.79 = (f32[24]{0:T(128)S(1)}, f32[24]{0:T(128)}, u32[]{:S(2)}) copy-start(f32[24]{0:T(128)} %get-tuple-element.179) | copy-start | bytes 292
  130.9 3.8 %copy-start.45 = (f32[1536]{0:T(1024)S(1)}, f32[1536]{0:T(1024)}, u32[]{:S(2)}) copy-start(f32[1536]{0:T(1024)} %get-tuple-element.163) | copy-start | bytes 18436
  131.0 4.0 %copy-start.75 = (f32[24]{0:T(128)S(1)}, f32[24]{0:T(128)}, u32[]{:S(2)}) copy-start(f32[24]{0:T(128)} %get-tuple-element.165) | copy-start | bytes 292
  258.0 3.2 %copy-start.5 = (f32[384,768]{1,0:T(8,128)S(1)}, f32[384,768]{1,0:T(8,128)}, u32[]{:S(2)}) copy-start(f32[384,768]{1,0:T(8,128)} %get-tuple-element.31.refs_1_) | copy-start | bytes 3538948
  258.0 15.6 %copy-start.60 = (f32[256]{0:T(256)S(1)}, f32[256]{0:T(256)}, u32[]{:S(2)}) copy-start(f32[256]{0:T(256)} %copy-done.59) | copy-start | bytes 3076
  258.0 15.8 %copy-start = (f32[192,3352]{1,0:T(8,128)S(1)}, f32[192,3352]{1,0:T(8,128)}, u32[]{:S(2)}) copy-start(f32[192,3352]{1,0:T(8,128)} %refs_3_.2) | copy-start | bytes 7723012
  258.0 15.8 %copy-start.8 = (f32[192,128]{1,0:T(8,128)S(1)}, f32[192,128]{1,0:T(8,128)}, u32[]{:S(2)}) copy-start(f32[192,128]{1,0:T(8,128)} %get-tuple-element.29.refs_2_) | copy-start | bytes 294916
  273.7 13.3 %copy-start.35 = (f32[5,448]{1,0:T(8,128)}, f32[5,448]{1,0:T(8,128)S(1)}, u32[]{:S(2)}) copy-start(f32[5,448]{1,0:T(8,128)S(1)} %reshape.714) | copy-start | bytes 26884
  273.8 14.6 %copy-start.63 = (f32[3,6]{1,0:T(4,128)}, f32[3,6]{1,0:T(4,128)S(1)}, u32[]{:S(2)}) copy-start(f32[3,6]{1,0:T(4,128)S(1)} %reshape.715) | copy-start | bytes 220
  275.5 2.5 copy-start.2
  278.0 5.9 %copy-start.4 = (f32[384,768]{1,0:T(8,128)S(1)}, f32[384,768]{1,0:T(8,128)}, u32[]{:S(2)}) copy-start(f32[384,768]{1,0:T(8,128)} %refs_2_.1) | copy-start | bytes 3538948
  278.0 5.9 %copy-start.6 = (f32[384,768]{1,0:T(8,128)S(1)}, f32[384,768]{1,0:T(8,128)}, u32[]{:S(2)}) copy-start(f32[384,768]{1,0:T(8,128)} %get-tuple-element.31.refs_1_) | copy-start | bytes 3538948
  278.0 5.9 %copy-start.7 = (f32[2,384,768]{2,1,0:T(8,128)S(1)}, f32[2,384,768]{2,1,0:T(8,128)}, u32[]{:S(2)}) copy-start(f32[2,384,768]{2,1,0:T(8,128)} %refs_3_.3) | copy-start | bytes 7077892
  283.9 3.1 %copy-start.37 = (f32[5,448]{1,0:T(8,128)S(1)}, f32[5,448]{1,0:T(8,128)}, u32[]{:S(2)}) copy-start(f32[5,448]{1,0:T(8,128)} %param.20) | copy-start | bytes 26884
  283.9 4.5 %copy-start.51 = (f32[1,3,6]{2,0,1:T(1,128)S(1)}, f32[1,3,6]{2,0,1:T(1,128)}, u32[]{:S(2)}) copy-start(f32[1,3,6]{2,0,1:T(1,128)} %get-tuple-element.193) | copy-start | bytes 220
  283.9 4.4 %copy-start.52 = (f32[1,3,6]{2,0,1:T(1,128)S(1)}, f32[1,3,6]{2,0,1:T(1,128)}, u32[]{:S(2)}) copy-start(f32[1,3,6]{2,0,1:T(1,128)} %get-tuple-element.194) | copy-start | bytes 220
  284.0 4.4 %copy-start.65 = (f32[3,6]{1,0:T(4,128)S(1)}, f32[3,6]{1,0:T(4,128)}, u32[]{:S(2)}) copy-start(f32[3,6]{1,0:T(4,128)} %param.21) | copy-start | bytes 220
  284.0 5.6 %copy-start.61 = (f32[384]{0:T(512)S(1)}, f32[384]{0:T(512)}, u32[]{:S(2)}) copy-start(f32[384]{0:T(512)} %get-tuple-element.153) | copy-start | bytes 4612
  284.0 5.6 %copy-start.62 = (f32[384]{0:T(512)S(1)}, f32[384]{0:T(512)}, u32[]{:S(2)}) copy-start(f32[384]{0:T(512)} %get-tuple-element.154) | copy-start | bytes 4612
  284.0 5.6 %copy-start.67 = (f32[384]{0:T(512)S(1)}, f32[384]{0:T(512)}, u32[]{:S(2)}) copy-start(f32[384]{0:T(512)} %param.22) | copy-start | bytes 4612
  284.0 6.3 %copy-start.28 = (bf16[1,256,768]{2,1,0:T(8,128)(2,1)S(1)}, bf16[1,256,768]{2,1,0:T(8,128)(2,1)}, u32[]{:S(2)}) copy-start(bf16[1,256,768]{2,1,0:T(8,128)(2,1)} %param.17) | copy-start | bytes 1179652
  284.0 6.3 %copy-start.30 = (f32[256,768]{1,0:T(8,128)S(1)}, f32[256,768]{1,0:T(8,128)}, u32[]{:S(2)}) copy-start(f32[256,768]{1,0:T(8,128)} %get-tuple-element.206) | copy-start | bytes 2359300
  286.9 4.6 %copy-start.71 = (f32[1,192]{1,0:T(1,128)S(1)}, f32[1,192]{1,0:T(1,128)}, u32[]{:S(2)}) copy-start(f32[1,192]{1,0:T(1,128)} %get-tuple-element.197) | copy-start | bytes 2308
  286.9 4.6 %copy-start.72 = (f32[1,192]{1,0:T(1,128)S(1)}, f32[1,192]{1,0:T(1,128)}, u32[]{:S(2)}) copy-start(f32[1,192]{1,0:T(1,128)} %get-tuple-element.198) | copy-start | bytes 2308
  286.9 4.6 %copy-start.78 = (f32[192]{0:T(256)S(1)}, f32[192]{0:T(256)}, u32[]{:S(2)}) copy-start(f32[192]{0:T(256)} %param.18) | copy-start | bytes 2308
  286.9 6.3 %copy-start.10 = (f32[1,256,1536]{1,2,0:T(8,128)S(1)}, f32[1,256,1536]{1,2,0:T(8,128)}, u32[]{:S(2)}) copy-start(f32[1,256,1536]{1,2,0:T(8,128)} %get-tuple-element.175) | copy-start | bytes 4718596
  286.9 6.3 %copy-start.41 = (f32[256]{0:T(256)S(1)}, f32[256]{0:T(256)}, u32[]{:S(2)}) copy-start(f32[256]{0:T(256)} %copy-done.40) | copy-start | bytes 3076
  (21 other events, 32.6 us)
Sparse Core Ops, SparseCore 0:
  10.4 43.7 all-gather.5
  56.3 24.0 all-gather.7
